TPU v7x, 128 devices: a whole 4x4x4 slice. The times are simulated.
128 devices in a mesh: dp: 2 (over z_hi), tile: 64 (over x, z_lo, y, core).
Axes of the slice: x: 4, y: 4, z: 4 (z_hi: 2, z_lo: 2; z = z_hi * 2 + z_lo), core: 2. Of those that a mesh axis runs over, the one named last changes fastest.
Arguments:
- inputs: bfloat16 [2, 1024, 8, 8, 128], P('dp', 'tile'), may hold values from -6 to 6
- cotangent: bfloat16 [2, 1024, 4, 4, 128], P('dp', 'tile'), may hold values from -6 to 6
- w_first: bfloat16 [1152, 128], replicated, may hold values from -0.1875 to 0.1875
- w_second: bfloat16 [1152, 128], replicated, may hold values from -0.1875 to 0.1875
- w_down: bfloat16 [512, 128], replicated, may hold values from -0.25 to 0.25
- edge_owner: int32 [1024, 4], replicated, may hold values from 0 to 63, all different within a row; in each aligned block of 16 rows (0 to 15, 16 to 31, ...) at most 2 rows name the same one
- corner_owner: int32 [1024, 4], replicated, may hold values from 0 to 63, all different within a row; in each aligned block of 16 rows (0 to 15, 16 to 31, ...) at most 2 rows name the same one
- neighbour_tile: int32 [1024, 8], replicated, may hold values from 0 to 15
- seam_rotation: int32 [1024, 8], replicated, may hold values from 0 to 3
Outputs:
- features: bfloat16 [2, 1024, 4, 4, 128], P('dp', 'tile')
- input_grad: float32 [2, 1024, 8, 8, 128], P('dp', 'tile')
- grad_first: float32 [1152, 128], P('dp')
- grad_second: float32 [1152, 128], P('dp')
- grad_down: float32 [512, 128], P('dp')
Inputs may be any that keep to these rules, and one draw needn't show every extreme that they name: `edge_owner`: the four devices of a row differ. Among the rows of the 16 tiles of one device no device is named more than 2 times, and some device exactly 2 times. `corner_owner`: as for edge_owner.
All inputs are finite; a program needn't handle non-finite values.
Results may differ from a plain program's by a relative error of at most 0.0085.
Values may be sent and summed in bfloat16 or wider, within the bound.
A program may use at most 64 MiB of HBM per device.

v0:
```python
import jax
import jax.numpy as jnp
import numpy as np
from jax import lax
from jax.sharding import PartitionSpec as P


def pixel_tables(side_len):
    pixel_grid = np.arange(side_len * side_len).reshape(side_len, side_len)
    edge_table = np.zeros((4, 4, side_len), np.int32)
    corner_table = np.zeros((4, 4), np.int32)
    turned = pixel_grid
    for quarter in range(4):
        edge_table[0, quarter] = turned[side_len - 1, :]
        edge_table[1, quarter] = turned[:, 0]
        edge_table[2, quarter] = turned[0, :]
        edge_table[3, quarter] = turned[:, side_len - 1]
        corner_table[0, quarter] = turned[side_len - 1, 0]
        corner_table[1, quarter] = turned[0, 0]
        corner_table[2, quarter] = turned[0, side_len - 1]
        corner_table[3, quarter] = turned[side_len - 1, side_len - 1]
        turned = turned.T[::-1, :]
    return (jnp.asarray(edge_table), jnp.asarray(corner_table))


def sender_plan(owners, rotation, local_ids, this_dev, devices, per_dev, slots):
    matched = (owners.reshape(devices, per_dev, 4) == this_dev).astype(jnp.int32)
    has_req = jnp.sum(matched, axis=2)
    before = jnp.cumsum(has_req, axis=1) - has_req
    slot_ids = jnp.arange(slots, dtype=jnp.int32)
    picked = has_req[:, :, None] * (before[:, :, None] == slot_ids[None, None, :]).astype(jnp.int32)
    is_valid = jnp.sum(picked, axis=1)
    tile_pos = jnp.arange(per_dev, dtype=jnp.int32)
    which_tile = jnp.sum(picked * tile_pos[None, :, None], axis=1)
    dir_ids = jnp.arange(4, dtype=jnp.int32)
    direction = jnp.sum(matched * dir_ids[None, None, :], axis=2)
    turn_count = jnp.sum(matched * rotation.reshape(devices, per_dev, 4), axis=2)
    source = jnp.sum(matched * local_ids.reshape(devices, per_dev, 4), axis=2)
    pick_dir = jnp.take_along_axis(direction, which_tile, axis=1)
    pick_turn = jnp.take_along_axis(turn_count, which_tile, axis=1)
    pick_src = jnp.take_along_axis(source, which_tile, axis=1)
    return (is_valid, pick_dir, pick_turn, pick_src)


def receiver_slots(owners, this_dev, per_dev, slots):
    my_rows = lax.dynamic_slice_in_dim(owners, this_dev * per_dev, per_dev, 0)
    shared = jnp.any(my_rows[:, :, None, None] == my_rows[None, None, :, :], axis=3).astype(
        jnp.int32
    )
    tile_pos = jnp.arange(per_dev, dtype=jnp.int32)
    earlier = (tile_pos[None, None, :] < tile_pos[:, None, None]).astype(jnp.int32)
    slot_rank = jnp.sum(shared * earlier, axis=2)
    return my_rows * slots + slot_rank


def make_plan(edge_owner, corner_owner, neighbour_tile, seam_rotation, per_dev, side_len):
    devices = lax.axis_size("tile")
    this_dev = lax.axis_index("tile")
    slots = max(2, 4 * per_dev // devices + 1)
    edge_send = sender_plan(
        edge_owner, seam_rotation[:, :4], neighbour_tile[:, :4], this_dev, devices, per_dev, slots
    )
    corner_send = sender_plan(
        corner_owner, seam_rotation[:, 4:], neighbour_tile[:, 4:], this_dev, devices, per_dev, slots
    )
    edge_recv = receiver_slots(edge_owner, this_dev, per_dev, slots)
    corner_recv = receiver_slots(corner_owner, this_dev, per_dev, slots)
    edge_table, corner_table = pixel_tables(side_len)
    return (edge_send, corner_send, edge_recv, corner_recv, edge_table, corner_table)


def fetch_rims(tiles, plan):
    edge_send, corner_send, edge_recv, corner_recv, edge_table, corner_table = plan
    per_dev = tiles.shape[0]
    side_len = tiles.shape[1]
    channels = tiles.shape[3]
    tile_pixels = tiles.reshape(per_dev, side_len * side_len, channels)
    edge_ok, edge_dir, edge_turn, edge_src = edge_send
    corner_ok, corner_dir, corner_turn, corner_src = corner_send
    edge_pix = edge_table[edge_dir, edge_turn]
    edge_vals = tile_pixels[edge_src[:, :, None], edge_pix]
    edge_vals = jnp.where(edge_ok[:, :, None, None] > 0, edge_vals, jnp.zeros_like(edge_vals))
    corner_pix = corner_table[corner_dir, corner_turn]
    corner_vals = tile_pixels[corner_src, corner_pix]
    corner_vals = jnp.where(corner_ok[:, :, None] > 0, corner_vals, jnp.zeros_like(corner_vals))
    got_edges, got_corners = (
        lax.all_to_all(edge_vals, "tile", split_axis=0, concat_axis=0, tiled=True),
        lax.all_to_all(corner_vals, "tile", split_axis=0, concat_axis=0, tiled=True),
    )
    devices = got_edges.shape[0]
    slots = got_edges.shape[1]
    edge_rims = got_edges.reshape(devices * slots, side_len, channels)[edge_recv]
    corner_rims = got_corners.reshape(devices * slots, channels)[corner_recv]
    corner_cells = corner_rims[:, :, None, None, :]
    north_rim = edge_rims[:, 0][:, None]
    east_rim = edge_rims[:, 1][:, :, None]
    south_rim = edge_rims[:, 2][:, None]
    west_rim = edge_rims[:, 3][:, :, None]
    top_row = jnp.concatenate([corner_cells[:, 3], north_rim, corner_cells[:, 0]], axis=2)
    middle_band = jnp.concatenate([west_rim, tiles, east_rim], axis=2)
    bottom_row = jnp.concatenate([corner_cells[:, 2], south_rim, corner_cells[:, 1]], axis=2)
    return jnp.concatenate([top_row, middle_band, bottom_row], axis=1)


def return_rims(back_pad, plan):
    edge_send, corner_send, edge_recv, corner_recv, edge_table, corner_table = plan
    per_dev = back_pad.shape[0]
    side_len = back_pad.shape[1] - 2
    channels = back_pad.shape[3]
    edge_ok, edge_dir, edge_turn, edge_src = edge_send
    corner_ok, corner_dir, corner_turn, corner_src = corner_send
    devices = edge_ok.shape[0]
    slots = edge_ok.shape[1]
    edge_rims = jnp.stack(
        [
            back_pad[:, 0, 1 : side_len + 1],
            back_pad[:, 1 : side_len + 1, side_len + 1],
            back_pad[:, side_len + 1, 1 : side_len + 1],
            back_pad[:, 1 : side_len + 1, 0],
        ],
        axis=1,
    )
    corner_rims = jnp.stack(
        [
            back_pad[:, 0, side_len + 1],
            back_pad[:, side_len + 1, side_len + 1],
            back_pad[:, side_len + 1, 0],
            back_pad[:, 0, 0],
        ],
        axis=1,
    )
    edge_back = jnp.zeros((devices * slots, side_len, channels), jnp.float32)
    edge_back = edge_back.at[edge_recv.reshape(-1)].set(edge_rims.reshape(-1, side_len, channels))
    corner_back = jnp.zeros((devices * slots, channels), jnp.float32)
    corner_back = corner_back.at[corner_recv.reshape(-1)].set(corner_rims.reshape(-1, channels))
    edge_back = edge_back.reshape(devices, slots, side_len, channels)
    corner_back = corner_back.reshape(devices, slots, channels)
    got_edges, got_corners = (
        lax.all_to_all(
            edge_back.astype(jnp.bfloat16), "tile", split_axis=0, concat_axis=0, tiled=True
        ).astype(edge_back.dtype),
        lax.all_to_all(
            corner_back.astype(jnp.bfloat16), "tile", split_axis=0, concat_axis=0, tiled=True
        ).astype(corner_back.dtype),
    )
    area = side_len * side_len
    interior = back_pad[:, 1 : side_len + 1, 1 : side_len + 1].reshape(per_dev * area, channels)
    edge_index = (edge_src[:, :, None] * area + edge_table[edge_dir, edge_turn]).reshape(-1)
    interior = interior.at[edge_index].add(got_edges.reshape(-1, channels))
    corner_index = (corner_src * area + corner_table[corner_dir, corner_turn]).reshape(-1)
    interior = interior.at[corner_index].add(got_corners.reshape(-1, channels))
    return interior.reshape(per_dev, side_len, side_len, channels)


def conv_valid(region, weight):
    tile_count = region.shape[0]
    out_rows = region.shape[1] - 2
    out_cols = region.shape[2] - 2
    channels = region.shape[3]
    running = jnp.zeros((tile_count * out_rows * out_cols, channels), jnp.float32)
    for row_off in range(3):
        for col_off in range(3):
            tap_rows = region[
                :, row_off : row_off + out_rows, col_off : col_off + out_cols
            ].reshape(-1, channels)
            tap_start = (3 * row_off + col_off) * channels
            running = running + jnp.dot(
                tap_rows,
                weight[tap_start : tap_start + channels],
                preferred_element_type=jnp.float32,
            )
    return running.reshape(tile_count, out_rows, out_cols, channels)


def conv_layer(tiles, weight, plan):
    padded = fetch_rims(tiles, plan)
    result = conv_valid(padded, weight)
    return (result, padded)


def weight_grad(padded, slope):
    out_rows = slope.shape[1]
    channels = slope.shape[3]
    slope_rows = slope.reshape(-1, channels)
    pieces = []
    for row_off in range(3):
        for col_off in range(3):
            tap_rows = padded[
                :, row_off : row_off + out_rows, col_off : col_off + out_rows
            ].reshape(-1, channels)
            pieces.append(
                lax.dot_general(
                    tap_rows,
                    slope_rows,
                    (((0,), (0,)), ((), ())),
                    preferred_element_type=jnp.float32,
                )
            )
    return jnp.concatenate(pieces, axis=0)


def conv_adjoint(slope, weight):
    tile_count = slope.shape[0]
    out_rows = slope.shape[1]
    channels = slope.shape[3]
    slope_rows = slope.reshape(-1, channels)
    back_pad = jnp.zeros((tile_count, out_rows + 2, out_rows + 2, channels), jnp.float32)
    for row_off in range(3):
        for col_off in range(3):
            tap_start = (3 * row_off + col_off) * channels
            contrib = lax.dot_general(
                slope_rows,
                weight[tap_start : tap_start + channels],
                (((1,), (1,)), ((), ())),
                preferred_element_type=jnp.float32,
            )
            back_pad = back_pad.at[
                :, row_off : row_off + out_rows, col_off : col_off + out_rows
            ].add(contrib.reshape(tile_count, out_rows, out_rows, channels))
    return back_pad


def down_forward(hidden, w_down):
    tile_count = hidden.shape[0]
    half_side = hidden.shape[1] // 2
    channels = hidden.shape[3]
    blocks = hidden.reshape(tile_count, half_side, 2, half_side, 2, channels)
    running = jnp.zeros((tile_count * half_side * half_side, channels), jnp.float32)
    for row_off in range(2):
        for col_off in range(2):
            tap_rows = blocks[:, :, row_off, :, col_off].reshape(-1, channels)
            tap_start = (2 * row_off + col_off) * channels
            running = running + jnp.dot(
                tap_rows,
                w_down[tap_start : tap_start + channels],
                preferred_element_type=jnp.float32,
            )
    return running.reshape(tile_count, half_side, half_side, channels)


def down_adjoint(cot, w_down):
    tile_count = cot.shape[0]
    half_side = cot.shape[1]
    channels = cot.shape[3]
    cot_rows = cot.reshape(-1, channels)
    outer_list = []
    for row_off in range(2):
        inner_list = []
        for col_off in range(2):
            tap_start = (2 * row_off + col_off) * channels
            contrib = lax.dot_general(
                cot_rows,
                w_down[tap_start : tap_start + channels],
                (((1,), (1,)), ((), ())),
                preferred_element_type=jnp.float32,
            )
            inner_list.append(contrib.reshape(tile_count, half_side, half_side, channels))
        outer_list.append(jnp.stack(inner_list, axis=3))
    return jnp.stack(outer_list, axis=2).reshape(tile_count, 2 * half_side, 2 * half_side, channels)


def down_weight_grad(hidden, cot):
    tile_count = hidden.shape[0]
    half_side = hidden.shape[1] // 2
    channels = hidden.shape[3]
    blocks = hidden.reshape(tile_count, half_side, 2, half_side, 2, channels)
    cot_rows = cot.reshape(-1, channels)
    pieces = []
    for row_off in range(2):
        for col_off in range(2):
            tap_rows = blocks[:, :, row_off, :, col_off].reshape(-1, channels)
            pieces.append(
                lax.dot_general(
                    tap_rows, cot_rows, (((0,), (0,)), ((), ())), preferred_element_type=jnp.float32
                )
            )
    return jnp.concatenate(pieces, axis=0)


def silu_slope(values):
    logistic = jax.nn.sigmoid(values)
    return logistic * (1.0 + values * (1.0 - logistic))


def local(
    inputs,
    cotangent,
    w_first,
    w_second,
    w_down,
    edge_owner,
    corner_owner,
    neighbour_tile,
    seam_rotation,
):
    tiles_in = inputs[0]
    per_dev = tiles_in.shape[0]
    side_len = tiles_in.shape[1]
    plan = make_plan(edge_owner, corner_owner, neighbour_tile, seam_rotation, per_dev, side_len)
    pre_first, pad_inputs = conv_layer(tiles_in, w_first, plan)
    hidden_first = jax.nn.silu(pre_first).astype(jnp.bfloat16)
    pre_second, pad_hidden = conv_layer(hidden_first, w_second, plan)
    hidden_second = jax.nn.silu(pre_second).astype(jnp.bfloat16)
    features = down_forward(hidden_second, w_down).astype(jnp.bfloat16)
    cot = cotangent[0]
    grad_scale = float(
        lax.axis_size("dp") * lax.axis_size("tile") * per_dev * side_len * side_len
    ) ** (-0.5)
    grad_low = down_weight_grad(hidden_second, cot) * grad_scale
    back_second = down_adjoint(cot, w_down)
    slope_second = (back_second * silu_slope(pre_second)).astype(jnp.bfloat16)
    grad_two = weight_grad(pad_hidden, slope_second) * grad_scale
    back_first = return_rims(conv_adjoint(slope_second, w_second), plan)
    slope_first = (back_first * silu_slope(pre_first)).astype(jnp.bfloat16)
    grad_one = weight_grad(pad_inputs, slope_first) * grad_scale
    input_grad = return_rims(conv_adjoint(slope_first, w_first), plan)
    summed = lax.psum((grad_one, grad_two, grad_low), "tile")
    reduced = (
        lax.psum_scatter(
            summed[0].astype(jnp.bfloat16), "dp", scatter_dimension=0, tiled=True
        ).astype(jnp.float32),
        lax.psum_scatter(
            summed[1].astype(jnp.bfloat16), "dp", scatter_dimension=0, tiled=True
        ).astype(jnp.float32),
        lax.psum_scatter(
            summed[2].astype(jnp.bfloat16), "dp", scatter_dimension=0, tiled=True
        ).astype(jnp.float32),
    )
    return (features[None], input_grad[None], reduced[0], reduced[1], reduced[2])


def solution(mesh):
    return jax.shard_map(
        local,
        mesh=mesh,
        in_specs=(
            P("dp", "tile", None, None, None),
            P("dp", "tile", None, None, None),
            P(),
            P(),
            P(),
            P(),
            P(),
            P(),
            P(),
        ),
        out_specs=(
            P("dp", "tile", None, None, None),
            P("dp", "tile", None, None, None),
            P("dp", None),
            P("dp", None),
            P("dp", None),
        ),
        check_vma=False,
    )
```

profile of v0, /device:TPU:1, one launch (start us, length us, event | category | flops | bytes accessed | tf_op | source)
XLA Modules:
  0.0 570.2 jit_solution(4695730579302962216)
XLA Ops:
  18.5 10.3 %all-to-all-start = ((bf16[64,2,128]{2,1,0:T(2,128)(2,1)}), bf16[64,2,128]{2,1,0:T(2,128)(2,1)S(1)}, u32[]{:S(2)}, u32[]{:S(2)}) async-start(bf16[64,2,128]{2,1,0:T(2,128)(2,1)} %broadcast_select_fusion.3), calls=%async_computation | async-start | bytes 65536 | tf_op jit(solution)/shard_map/all_to_all | solution.py:88
  37.7 5.8 %gather_fusion.4 = bf16[1024,128]{1,0:T(8,128)(2,1)S(1)} fusion(bf16[16,64,128]{2,1,0:T(8,128)(2,1)S(1)} %bitcast.467, s32[1024]{0:T(1024)S(1)} %reshape.1301), kind=kCustom, calls=%fused_computation.10 | custom fusion | bytes 532480 | tf_op jit(solution)/shard_map/gather | solution.py:81
  52.3 9.1 %all-to-all-start.1 = ((bf16[64,2,8,128]{3,2,1,0:T(8,128)(2,1)}), bf16[64,2,8,128]{3,2,1,0:T(8,128)(2,1)S(1)}, u32[]{:S(2)}, u32[]{:S(2)}) async-start(bf16[64,2,8,128]{3,2,1,0:T(8,128)(2,1)} %broadcast_select_fusion.1), calls=%async_computation.1 | async-start | bytes 524288 | tf_op jit(solution)/shard_map/all_to_all | solution.py:87
  62.4 8.7 %all-to-all-done.1 = bf16[64,2,8,128]{3,2,1,0:T(8,128)(2,1)S(1)} async-done(((bf16[64,2,8,128]{3,2,1,0:T(8,128)(2,1)}), bf16[64,2,8,128]{3,2,1,0:T(8,128)(2,1)S(1)}, u32[]{:S(2)}, u32[]{:S(2)}) %all-to-all-start.1) | async-done | bytes 262176 | tf_op jit(solution)/shard_map/all_to_all | solution.py:87
  76.6 5.8 %gather_fusion.8 = bf16[1024,128]{1,0:T(8,128)(2,1)S(1)} fusion(bf16[16,64,128]{2,1,0:T(8,128)(2,1)S(1)} %multiply_convert_fusion.7, s32[1024]{0:T(1024)S(1)} %reshape.1301), kind=kCustom, calls=%fused_computation.14 | custom fusion | bytes 532480 | tf_op jit(solution)/shard_map/gather | solution.py:81
  84.4 4.5 all-to-all-start.2
  89.8 6.9 %all-to-all-done.2 = bf16[64,2,128]{2,1,0:T(2,128)(2,1)S(1)} async-done(((bf16[64,2,128]{2,1,0:T(2,128)(2,1)}), bf16[64,2,128]{2,1,0:T(2,128)(2,1)S(1)}, u32[]{:S(2)}, u32[]{:S(2)}) %all-to-all-start.2) | async-done | bytes 32800 | tf_op jit(solution)/shard_map/all_to_all | solution.py:88
  96.7 5.0 all-to-all-start.3
  102.8 8.6 %all-to-all-done.3 = bf16[64,2,8,128]{3,2,1,0:T(8,128)(2,1)S(1)} async-done(((bf16[64,2,8,128]{3,2,1,0:T(8,128)(2,1)}), bf16[64,2,8,128]{3,2,1,0:T(8,128)(2,1)S(1)}, u32[]{:S(2)}, u32[]{:S(2)}) %all-to-all-start.3) | async-done | bytes 262176 | tf_op jit(solution)/shard_map/all_to_all | solution.py:87
  122.6 5.1 scatter-add.89
  127.7 2.9 fusion.5
  130.6 5.1 scatter-add.90
  137.0 3.8 scatter-add.94
  141.9 3.8 scatter-add.95
  147.1 3.8 scatter-add.99
  151.7 3.1 scatter-add.100
  166.6 4.9 scatter_fusion
  172.3 4.7 all-to-all-start.4
  181.8 5.0 all-to-all-done.4
  186.8 4.5 all-to-all-start.5
  192.2 6.4 %scatter_custom_fusion.1 = f32[1024,128]{1,0:T(8,128)S(1)} fusion(f32[1024,128]{1,0:T(8,128)S(1)} %bitcast.493, s32[1024]{0:T(1024)} %bitcast.645, bf16[1024,128]{1,0:T(8,128)(2,1)S(1)} %bitcast.515), kind=kCustom, calls=%fused_computation.109 | custom fusion | flops 262144 | bytes 786432 | tf_op jit(solution)/shard_map/scatter-add | solution.py:149
  205.3 289.4 %all-reduce.4 = (bf16[1152,128]{1,0:T(8,128)(2,1)}, bf16[1152,128]{1,0:T(8,128)(2,1)}, bf16[512,128]{1,0:T(8,128)(2,1)}) all-reduce(f32[1152,128]{1,0:T(8,128)S(1)} %broadcast_multiply_fusion.1, f32[1152,128]{1,0:T(8,128)S(1)} %broadcast_multiply_fusion, f32[512,128]{1,0:T(8,128)S(1)} %copy-done.10), channel_id=1, replica_groups=mesh['dp'=2,'tile'=64] {'tile'}, use_global_device_ids=true, to_apply=%region_27.29 | all-reduce | flops 360448 | bytes 2162688 | tf_op jit(solution)/shard_map/psum | solution.py:317
  496.8 3.9 scatter-add.106
  502.9 4.0 scatter-add.109
  507.3 2.7 scatter-add.133
  510.3 2.7 scatter-add.134
  513.5 2.7 scatter-add.136
  517.0 2.7 scatter-add.137
  523.7 10.7 %all-to-all-start.6 = ((bf16[64,2,8,128]{3,2,1,0:T(8,128)(2,1)}), bf16[64,2,8,128]{3,2,1,0:T(8,128)(2,1)S(1)}, u32[]{:S(2)}, u32[]{:S(2)}) async-start(bf16[64,2,8,128]{3,2,1,0:T(8,128)(2,1)} %bitcast.139), calls=%async_computation.6 | async-start | bytes 524288 | tf_op jit(solution)/shard_map/all_to_all | solution.py:139
  536.0 8.3 %all-to-all-done.6 = bf16[64,2,8,128]{3,2,1,0:T(8,128)(2,1)S(1)} async-done(((bf16[64,2,8,128]{3,2,1,0:T(8,128)(2,1)}), bf16[64,2,8,128]{3,2,1,0:T(8,128)(2,1)S(1)}, u32[]{:S(2)}, u32[]{:S(2)}) %all-to-all-start.6) | async-done | bytes 262176 | tf_op jit(solution)/shard_map/all_to_all | solution.py:139
  544.4 4.5 all-to-all-start.7
  550.5 6.4 %scatter_custom_fusion.5 = f32[1024,128]{1,0:T(8,128)S(1)} fusion(f32[1024,128]{1,0:T(8,128)S(1)} %bitcast.551, s32[1024]{0:T(1024)} %bitcast.646, bf16[1024,128]{1,0:T(8,128)(2,1)S(1)} %bitcast.516), kind=kCustom, calls=%fused_computation.107 | custom fusion | flops 262144 | bytes 786432 | tf_op jit(solution)/shard_map/scatter-add | solution.py:149
  (404 shorter events, 98.0 us)
Async XLA Ops:
  14.6 15.8 %copy-start.3 = (bf16[1,16,4,4,128]{4,3,2,1,0:T(4,128)(2,1)S(1)}, bf16[1,16,4,4,128]{4,3,2,1,0:T(4,128)(2,1)}, u32[]{:S(2)}) copy-start(bf16[1,16,4,4,128]{4,3,2,1,0:T(4,128)(2,1)} %param.50) | copy-start | bytes 196612
  14.6 15.8 %copy-start.20 = (bf16[512,128]{1,0:T(8,128)(2,1)S(1)}, bf16[512,128]{1,0:T(8,128)(2,1)}, u32[]{:S(2)}) copy-start(bf16[512,128]{1,0:T(8,128)(2,1)} %param.53) | copy-start | bytes 393220
  18.5 33.8 %all-to-all-start = ((bf16[64,2,128]{2,1,0:T(2,128)(2,1)}), bf16[64,2,128]{2,1,0:T(2,128)(2,1)S(1)}, u32[]{:S(2)}, u32[]{:S(2)}) async-start(bf16[64,2,128]{2,1,0:T(2,128)(2,1)} %broadcast_select_fusion.3), calls=%async_computation | async-start | bytes 65536 | tf_op jit(solution)/shard_map/all_to_all | solution.py:88
  37.7 12.8 %copy-start.59 = (s32[4]{0:T(128)S(1)}, s32[4]{0:T(128)}, u32[]{:S(2)}) copy-start(s32[4]{0:T(128)} %constant.526.clone.1) | copy-start | bytes 52
  52.3 18.8 %all-to-all-start.1 = ((bf16[64,2,8,128]{3,2,1,0:T(8,128)(2,1)}), bf16[64,2,8,128]{3,2,1,0:T(8,128)(2,1)S(1)}, u32[]{:S(2)}, u32[]{:S(2)}) async-start(bf16[64,2,8,128]{3,2,1,0:T(8,128)(2,1)} %broadcast_select_fusion.1), calls=%async_computation.1 | async-start | bytes 524288 | tf_op jit(solution)/shard_map/all_to_all | solution.py:87
  61.6 10.3 %copy-start.4 = (bf16[1,16,8,8,128]{4,1,3,2,0:T(8,128)(2,1)}, bf16[1,16,8,8,128]{4,1,3,2,0:T(8,128)(2,1)S(1)}, u32[]{:S(2)}) copy-start(bf16[1,16,8,8,128]{4,1,3,2,0:T(8,128)(2,1)S(1)} %copy.394) | copy-start | bytes 786436
  62.3 9.7 %copy-start.42 = (bf16[16,1,1,1,128]{4,0,3,2,1:T(8,128)(2,1)}, bf16[16,1,1,1,128]{4,0,3,2,1:T(8,128)(2,1)S(1)}, u32[]{:S(2)}) copy-start(bf16[16,1,1,1,128]{4,0,3,2,1:T(8,128)(2,1)S(1)} %copy.403) | copy-start | bytes 12292
  62.3 9.7 %copy-start.44 = (bf16[16,1,1,1,128]{4,0,3,2,1:T(8,128)(2,1)}, bf16[16,1,1,1,128]{4,0,3,2,1:T(8,128)(2,1)S(1)}, u32[]{:S(2)}) copy-start(bf16[16,1,1,1,128]{4,0,3,2,1:T(8,128)(2,1)S(1)} %copy.404) | copy-start | bytes 12292
  62.4 9.6 %copy-start.46 = (bf16[16,1,1,1,128]{4,0,3,2,1:T(8,128)(2,1)}, bf16[16,1,1,1,128]{4,0,3,2,1:T(8,128)(2,1)S(1)}, u32[]{:S(2)}) copy-start(bf16[16,1,1,1,128]{4,0,3,2,1:T(8,128)(2,1)S(1)} %copy.405) | copy-start | bytes 12292
  62.4 9.6 %copy-start.48 = (bf16[16,1,1,1,128]{4,0,3,2,1:T(8,128)(2,1)}, bf16[16,1,1,1,128]{4,0,3,2,1:T(8,128)(2,1)S(1)}, u32[]{:S(2)}) copy-start(bf16[16,1,1,1,128]{4,0,3,2,1:T(8,128)(2,1)S(1)} %copy.406) | copy-start | bytes 12292
  84.4 12.3 %all-to-all-start.2 = ((bf16[64,2,128]{2,1,0:T(2,128)(2,1)}), bf16[64,2,128]{2,1,0:T(2,128)(2,1)S(1)}, u32[]{:S(2)}, u32[]{:S(2)}) async-start(bf16[64,2,128]{2,1,0:T(2,128)(2,1)} %broadcast_select_fusion.2), calls=%async_computation.2 | async-start | bytes 65536 | tf_op jit(solution)/shard_map/all_to_all | solution.py:88
  96.7 14.8 %all-to-all-start.3 = ((bf16[64,2,8,128]{3,2,1,0:T(8,128)(2,1)}), bf16[64,2,8,128]{3,2,1,0:T(8,128)(2,1)S(1)}, u32[]{:S(2)}, u32[]{:S(2)}) async-start(bf16[64,2,8,128]{3,2,1,0:T(8,128)(2,1)} %broadcast_select_fusion), calls=%async_computation.3 | async-start | bytes 524288 | tf_op jit(solution)/shard_map/all_to_all | solution.py:87
  102.8 9.7 %copy-start.50 = (bf16[16,1,1,1,128]{4,0,3,2,1:T(8,128)(2,1)}, bf16[16,1,1,1,128]{4,0,3,2,1:T(8,128)(2,1)S(1)}, u32[]{:S(2)}) copy-start(bf16[16,1,1,1,128]{4,0,3,2,1:T(8,128)(2,1)S(1)} %copy.399) | copy-start | bytes 12292
  102.8 9.7 %copy-start.52 = (bf16[16,1,1,1,128]{4,0,3,2,1:T(8,128)(2,1)}, bf16[16,1,1,1,128]{4,0,3,2,1:T(8,128)(2,1)S(1)}, u32[]{:S(2)}) copy-start(bf16[16,1,1,1,128]{4,0,3,2,1:T(8,128)(2,1)S(1)} %copy.400) | copy-start | bytes 12292
  102.8 9.6 %copy-start.54 = (bf16[16,1,1,1,128]{4,0,3,2,1:T(8,128)(2,1)}, bf16[16,1,1,1,128]{4,0,3,2,1:T(8,128)(2,1)S(1)}, u32[]{:S(2)}) copy-start(bf16[16,1,1,1,128]{4,0,3,2,1:T(8,128)(2,1)S(1)} %copy.401) | copy-start | bytes 12292
  102.8 9.6 %copy-start.56 = (bf16[16,1,1,1,128]{4,0,3,2,1:T(8,128)(2,1)}, bf16[16,1,1,1,128]{4,0,3,2,1:T(8,128)(2,1)S(1)}, u32[]{:S(2)}) copy-start(bf16[16,1,1,1,128]{4,0,3,2,1:T(8,128)(2,1)S(1)} %copy.402) | copy-start | bytes 12292
  155.4 6.1 %copy-start.6 = (f32[16,4,2,4,2,128]{5,0,4,3,2,1:T(8,128)S(1)}, f32[16,4,2,4,2,128]{5,0,4,3,2,1:T(8,128)}, u32[]{:S(2)}) copy-start(f32[16,4,2,4,2,128]{5,0,4,3,2,1:T(8,128)} %copy.280) | copy-start | bytes 1572868
  166.6 13.7 %copy-start.17 = (bf16[16,4,1,4,1,128]{5,3,1,0,4,2:T(4,128)(2,1)S(1)}, bf16[16,4,1,4,1,128]{5,3,1,0,4,2:T(4,128)(2,1)}, u32[]{:S(2)}) copy-start(bf16[16,4,1,4,1,128]{5,3,1,0,4,2:T(4,128)(2,1)} %copy-done.16) | copy-start | bytes 196612
  172.2 19.1 %copy-start.30 = (f32[128,128]{1,0:T(8,128)S(1)}, f32[128,128]{1,0:T(8,128)}, u32[]{:S(2)}) copy-start(f32[128,128]{1,0:T(8,128)} %fusion.174) | copy-start | bytes 196612
  172.2 19.1 %copy-start.31 = (f32[128,128]{1,0:T(8,128)S(1)}, f32[128,128]{1,0:T(8,128)}, u32[]{:S(2)}) copy-start(f32[128,128]{1,0:T(8,128)} %fusion.175) | copy-start | bytes 196612
  172.2 19.1 %copy-start.32 = (f32[128,128]{1,0:T(8,128)S(1)}, f32[128,128]{1,0:T(8,128)}, u32[]{:S(2)}) copy-start(f32[128,128]{1,0:T(8,128)} %fusion.176) | copy-start | bytes 196612
  172.2 19.1 %copy-start.33 = (f32[128,128]{1,0:T(8,128)S(1)}, f32[128,128]{1,0:T(8,128)}, u32[]{:S(2)}) copy-start(f32[128,128]{1,0:T(8,128)} %fusion.177) | copy-start | bytes 196612
  172.3 14.5 %all-to-all-start.4 = ((bf16[64,2,8,128]{3,2,1,0:T(8,128)(2,1)}), bf16[64,2,8,128]{3,2,1,0:T(8,128)(2,1)S(1)}, u32[]{:S(2)}, u32[]{:S(2)}) async-start(bf16[64,2,8,128]{3,2,1,0:T(8,128)(2,1)} %bitcast.518), calls=%async_computation.4 | async-start | bytes 524288 | tf_op jit(solution)/shard_map/all_to_all | solution.py:139
  186.8 12.3 %all-to-all-start.5 = ((bf16[64,2,128]{2,1,0:T(2,128)(2,1)}), bf16[64,2,128]{2,1,0:T(2,128)(2,1)S(1)}, u32[]{:S(2)}, u32[]{:S(2)}) async-start(bf16[64,2,128]{2,1,0:T(2,128)(2,1)} %bitcast.114), calls=%async_computation.5 | async-start | bytes 65536 | tf_op jit(solution)/shard_map/all_to_all | solution.py:142
  191.3 367.3 %reduce-scatter.8.cloned.1.call-start = ((), (), s32[]{:S(2)}) async-start(), calls=%async_computation.13 | async-start | bytes 196608 | tf_op jit(solution)/shard_map/reduce_scatter | solution.py:325
  204.4 290.6 %copy-start.9 = (bf16[1152,128]{1,0:T(8,128)(2,1)S(1)}, bf16[1152,128]{1,0:T(8,128)(2,1)}, u32[]{:S(2)}) copy-start(bf16[1152,128]{1,0:T(8,128)(2,1)} %param.51) | copy-start | bytes 884740
  494.7 65.4 %reduce-scatter.4.cloned.1.call-start = ((), (), s32[]{:S(2)}) async-start(), calls=%async_computation.11 | async-start | bytes 442368 | tf_op jit(solution)/shard_map/reduce_scatter | solution.py:319
  519.7 42.1 %reduce-scatter.6.cloned.1.call-start = ((), (), s32[]{:S(2)}) async-start(), calls=%async_computation.12 | async-start | bytes 442368 | tf_op jit(solution)/shard_map/reduce_scatter | solution.py:322
  520.6 28.3 %copy-start.15 = (bf16[16,4,1,4,1,128]{5,3,1,0,4,2:T(4,128)(2,1)S(1)}, bf16[16,4,1,4,1,128]{5,3,1,0,4,2:T(4,128)(2,1)}, u32[]{:S(2)}) copy-start(bf16[16,4,1,4,1,128]{5,3,1,0,4,2:T(4,128)(2,1)} %copy-done.14) | copy-start | bytes 196612
  520.6 28.3 %copy-start.21 = (f32[256,128]{1,0:T(8,128)S(1)}, f32[256,128]{1,0:T(8,128)}, u32[]{:S(2)}) copy-start(f32[256,128]{1,0:T(8,128)} %convolution_add_fusion.33) | copy-start | bytes 393220
  523.7 20.6 %all-to-all-start.6 = ((bf16[64,2,8,128]{3,2,1,0:T(8,128)(2,1)}), bf16[64,2,8,128]{3,2,1,0:T(8,128)(2,1)S(1)}, u32[]{:S(2)}, u32[]{:S(2)}) async-start(bf16[64,2,8,128]{3,2,1,0:T(8,128)(2,1)} %bitcast.139), calls=%async_computation.6 | async-start | bytes 524288 | tf_op jit(solution)/shard_map/all_to_all | solution.py:139
  544.4 12.6 %all-to-all-start.7 = ((bf16[64,2,128]{2,1,0:T(2,128)(2,1)}), bf16[64,2,128]{2,1,0:T(2,128)(2,1)S(1)}, u32[]{:S(2)}, u32[]{:S(2)}) async-start(bf16[64,2,128]{2,1,0:T(2,128)(2,1)} %bitcast.146), calls=%async_computation.7 | async-start | bytes 65536 | tf_op jit(solution)/shard_map/all_to_all | solution.py:142
  (39 other events, 50.8 us)
Sparse Core Ops, SparseCore 0:
  494.9 17.1 reduce-scatter.7
  519.8 18.9 reduce-scatter.3
  541.2 15.6 reduce-scatter.5
where the time goes:
time: 579 us; the launch traced here: 570 us
  blocking collectives  289 us (50%)
  local copies, waits for them, and re-layouts  99.7 us (17%)
  starting transfers between devices  53.7 us (9%)
  other arithmetic  38.7 us (7%)
  waiting for transfers between devices  38.6 us (7%)
  matrix products  34.1 us (6%)
  between operations  16 us (3%)
    psum x1, blocking collectives, local(): summed = lax.psum((grad_one, grad_two, grad_low), 'tile')  289 us
    scatter-add x14, local copies, waits for them, and re-layouts, conv_adjoint(): back_pad = back_pad.at[:, row_off:row_off + out_rows, col_off:col_off + o...  43.8 us
    all_to_all x2, waiting for transfers between devices, fetch_rims(): lax.all_to_all(edge_vals, 'tile', split_axis=0, concat_axis=0, tiled=True)  17.3 us
    all_to_all x2, starting transfers between devices, return_rims(): lax.all_to_all(edge_back.astype(jnp.bfloat16), 'tile', split_axis=0, conc...  15.4 us
    dot_general x18, matrix products, conv_adjoint(): lax.dot_general(slope_rows, weight[tap_start:tap_start + channels], (((1,...  15 us
    all_to_all x2, starting transfers between devices, fetch_rims(): lax.all_to_all(corner_vals, 'tile', split_axis=0, concat_axis=0, tiled=True)  14.9 us
    all_to_all x2, starting transfers between devices, fetch_rims(): lax.all_to_all(edge_vals, 'tile', split_axis=0, concat_axis=0, tiled=True)  14.2 us
    all_to_all x2, waiting for transfers between devices, return_rims(): lax.all_to_all(edge_back.astype(jnp.bfloat16), 'tile', split_axis=0, conc...  13.3 us
  transfers between devices with their start and end apart: 11, of which 6 were waited for; matrix products, arithmetic and copies ran while one was open for 14% of the time, Pallas kernels for 0%

commit v1 on v0

v1 whole, which is shorter than its diff:
```python
import jax
import jax.numpy as jnp
import numpy as np
from jax import lax
from jax.experimental import pallas as pl
from jax.experimental.pallas import tpu as pltpu
from jax.sharding import PartitionSpec as P

MESH = pl.DeviceIdType.MESH
F32 = jnp.float32
BF16 = jnp.bfloat16
N_TILE = 64
T = 16
S = 8
C = 128
PIX = S * S * T
TAPS = [(p, q) for p in range(3) for q in range(3)]
GRAD_SCALE = float(2 * 1024 * 64) ** -0.5
NB_LATE = (36 + 16, 36)


def seam_lines():
    grid = np.arange(S * S).reshape(S, S)
    first = np.zeros((8, 4), int)
    step = np.zeros((8, 4), int)
    for turn in range(4):
        turned = np.rot90(grid, turn)
        lines = [turned[-1, :], turned[:, 0], turned[0, :], turned[:, -1]]
        for k, line in enumerate(lines):
            first[k, turn], step[k, turn] = line[0], line[1] - line[0]
        cells = [turned[-1, 0], turned[0, 0], turned[0, -1], turned[-1, -1]]
        for k, cell in enumerate(cells):
            first[4 + k, turn] = cell
    return first, step


def iota(shape, axis):
    return lax.broadcasted_iota(jnp.int32, shape, axis)


def hot(mask):
    return jnp.where(mask, 1.0, 0.0).astype(BF16)


def mm(a, b):
    return jnp.dot(a, b, preferred_element_type=F32)


def mm_nt(a, b):
    return lax.dot_general(a, b, (((1,), (1,)), ((), ())), preferred_element_type=F32)


def kernel(
    x_ref, cot_ref, w1_ref, w2_ref, wd_ref, eo_ref, co_ref, nb_ref, rot_ref,
    feat_ref, ig_ref, o1_ref, o2_ref, od_ref,
    wide, bp, pre1, pad1, pad2, slope_pad, g_mat, gt_mat, gc_mat, gct_mat,
    r_mat, rt_mat, rc_mat, rct_mat, w1t, w2t, wdt, back2, hid2, cot_p, cot_t, slope_t,
    small, gf0, gf1, s_a0, s_a1, r_a0, r_a1, s_b, r_b, s_c, r_c0, r_c1,
    s_edge, r_edge, s_corner, r_corner,
    ex_send, ex_recv, red_send, red_recv,
):
    dp = lax.axis_index("dp")
    me = lax.axis_index("tile")
    core = lax.rem(me, 2)
    chip = dp * 32 + lax.div(me, 2)
    flat = dp * N_TILE + me
    barrier = pltpu.get_barrier_semaphore()

    def greet(o, carry):
        other = lax.rem(flat + o, 2 * N_TILE)
        pl.semaphore_signal(
            barrier, inc=1,
            device_id=(lax.div(other, N_TILE), lax.rem(other, N_TILE)), device_id_type=MESH,
        )
        return carry

    lax.fori_loop(1, 2 * N_TILE, greet, 0)

    me_f = me.astype(F32)
    own = jnp.concatenate([eo_ref[...], co_ref[...]], axis=0).astype(F32)
    src = nb_ref[...].astype(F32)
    rot = rot_ref[...].astype(F32)
    row8 = iota((8, 1024), 0)
    first, step = seam_lines()
    base_v = jnp.zeros((8, 1024), F32)
    step_v = jnp.zeros((8, 1024), F32)
    for turn in range(4):
        bcol = jnp.zeros((8, 1024), F32)
        scol = jnp.zeros((8, 1024), F32)
        for k in range(8):
            bcol = jnp.where(row8 == k, float(first[k, turn]), bcol)
            scol = jnp.where(row8 == k, float(step[k, turn]), scol)
        base_v = jnp.where(rot == float(turn), bcol, base_v)
        step_v = jnp.where(rot == float(turn), scol, step_v)
    match = jnp.where(own == me_f, 1.0, 0.0)

    def per_kind(v):
        a = jnp.broadcast_to(jnp.sum(v[0:4], axis=0, keepdims=True), (4, 1024))
        b = jnp.broadcast_to(jnp.sum(v[4:8], axis=0, keepdims=True), (4, 1024))
        return jnp.concatenate([a, b], axis=0)

    has = per_kind(match)
    lane16 = jnp.bitwise_and(iota((8, 1024), 1), 15)
    acc = has
    for sh in (1, 2, 4, 8):
        acc = acc + jnp.where(lane16 >= sh, pltpu.roll(acc, sh, 1), 0.0)
    rank = acc - has
    table = []
    for s in range(2):
        sel = match * jnp.where(rank == float(s), 1.0, 0.0)
        for v in (sel, sel * base_v, sel * step_v, sel * src):
            table.append(per_kind(v))
    tab = jnp.concatenate([v[0:1] for v in table] + [v[4:5] for v in table], axis=0).astype(BF16)
    lane_i = iota((1, 1024), 1)
    sub_i = iota((1024, 1), 0)
    lane_f = lane_i.astype(F32)
    sub_f = sub_i.astype(F32)
    blk_l = jnp.right_shift(lane_i, 4).astype(F32)
    blk_s = jnp.right_shift(sub_i, 4).astype(F32)
    block_diag = hot(blk_s == blk_l)
    slots_e = mm(tab, block_diag)
    pair_s = jnp.right_shift(iota((128, 1), 0), 1).astype(F32)
    slots_c = mm_nt(tab, hot(pair_s == blk_l))

    def target(rows, which, px):
        v0, b0, t0, n0, v1, b1, t1, n1 = [rows[i:i + 1] for i in range(8)]
        late = which > 0.5
        valid = jnp.where(late, v1, v0)
        pixel = jnp.where(late, b1, b0) + jnp.where(late, t1, t0) * px
        return jnp.where(valid > 0.5, pixel * float(T) + jnp.where(late, n1, n0), -1.0)

    te = target(
        slots_e[0:8],
        jnp.bitwise_and(jnp.right_shift(lane_i, 3), 1).astype(F32),
        jnp.bitwise_and(lane_i, 7).astype(F32),
    )
    tc = target(slots_c[8:16], jnp.bitwise_and(lane_i[:, :128], 1).astype(F32), 0.0)

    def as_column(row, n):
        return jnp.transpose(jnp.broadcast_to(row, (128, n)))[:, 0:1]

    g_mat[...] = hot(as_column(te, 1024) == lane_f)
    gc_mat[...] = hot(as_column(tc, 128) == lane_f)

    pad1[...] = jnp.zeros_like(pad1)
    wide[...] = x_ref[...].astype(F32)
    for px in range(S * S):
        pad1[1 + px // S, 1 + px % S] = wide[pl.ds(px, T, stride=S * S), :].astype(BF16)

    def pack(n, edges, corners):
        s_edge[n] = edges.astype(BF16).reshape(N_TILE, T, C)
        s_corner[n] = corners.astype(BF16).reshape(N_TILE, 2, C)

    def gather(n, field):
        pack(n, mm(g_mat[...], field), mm(gc_mat[...], field))

    def exchange(n, d):
        e = pltpu.make_async_remote_copy(
            src_ref=s_edge.at[n, d], dst_ref=r_edge.at[n, me],
            send_sem=ex_send.at[n, 0], recv_sem=ex_recv.at[n, 0],
            device_id=(dp, d), device_id_type=MESH,
        )
        c = pltpu.make_async_remote_copy(
            src_ref=s_corner.at[n, d], dst_ref=r_corner.at[n, me],
            send_sem=ex_send.at[n, 1], recv_sem=ex_recv.at[n, 1],
            device_id=(dp, d), device_id_type=MESH,
        )
        return e, c

    def ex_start(n):
        def send(o, carry):
            e, c = exchange(n, lax.rem(me + o, N_TILE))
            e.start()
            c.start()
            return carry

        lax.fori_loop(1, N_TILE, send, 0)
        r_edge[n, me] = s_edge[n, me]
        r_corner[n, me] = s_corner[n, me]

    def ex_all(n):
        rest = pl.ds(0, N_TILE - 1)
        to = (dp, lax.rem(me + 1, N_TILE))
        e = pltpu.make_async_remote_copy(
            src_ref=s_edge.at[n, rest], dst_ref=r_edge.at[n, rest],
            send_sem=ex_send.at[n, 0], recv_sem=ex_recv.at[n, 0],
            device_id=to, device_id_type=MESH,
        )
        c = pltpu.make_async_remote_copy(
            src_ref=s_corner.at[n, rest], dst_ref=r_corner.at[n, rest],
            send_sem=ex_send.at[n, 1], recv_sem=ex_recv.at[n, 1],
            device_id=to, device_id_type=MESH,
        )
        return e, c

    def ex_wait(n):
        e, c = ex_all(n)
        e.wait_recv()
        c.wait_recv()
        return r_edge[n].reshape(N_TILE * T, C), r_corner[n].reshape(2 * N_TILE, C)

    gather(0, pad1[1:9, 1:9].reshape(PIX, C))
    pl.semaphore_wait(barrier, 2 * N_TILE - 1)
    ex_start(0)

    ownb = own.astype(BF16)
    pick = hot(iota((128, 1), 0).astype(F32) + me_f * float(T) == lane_f)
    my_row = mm_nt(ownb, pick)
    my_col = mm_nt(pick[0:16], ownb)
    earlier = iota((T, 128), 1).astype(F32) < iota((T, 128), 0).astype(F32)

    def slot_base(kind, per_owner, per_rank):
        out = []
        for k in range(4 * kind, 4 * kind + 4):
            col = my_col[:, k:k + 1]
            shared = jnp.zeros((T, 128), F32)
            for k2 in range(4 * kind, 4 * kind + 4):
                shared = shared + jnp.where(col == my_row[k2:k2 + 1], 1.0, 0.0)
            rk = jnp.sum(jnp.where(earlier, shared, 0.0), axis=1, keepdims=True)
            out.append(col * per_owner + rk * per_rank)
        return out

    base_e = slot_base(0, 16.0, 8.0)
    base_c = slot_base(1, 2.0, 1.0)
    col_e = jnp.concatenate([b + float(px) for b in base_e for px in range(S)], axis=0)
    col_c = jnp.concatenate(base_c + [jnp.full((64, 1), -1.0, F32)], axis=0)
    r_mat[...] = hot(col_e == lane_f)
    rc_mat[...] = hot(col_c == lane_f[:, :128])
    row_e = jnp.transpose(jnp.broadcast_to(col_e, (512, 128)))[0:1]
    row_c = jnp.transpose(jnp.broadcast_to(col_c, (128, 128)))[0:1]
    rt_mat[...] = hot(sub_f == row_e)
    rct_mat[...] = hot(sub_f[:128] == row_c)
    gt_mat[...] = hot(sub_f == te)
    gct_mat[...] = hot(sub_f == tc)

    def flip(w):
        return jnp.transpose(w.astype(F32)).astype(BF16)

    for tap in range(9):
        at = slice(tap * C, tap * C + C)
        w1t[at] = flip(w1_ref[at])
        w2t[at] = flip(w2_ref[at])
    for tap in range(4):
        at = slice(tap * C, tap * C + C)
        wdt[at] = flip(wd_ref[at])
    small[...] = cot_ref[...].astype(F32)
    for px in range(16):
        cot_p[pl.ds(px * T, T), :] = small[pl.ds(px, T, stride=16), :].astype(BF16)
    cot_t[...] = flip(cot_p[...])
    for tap in range(4):
        back = mm(cot_p[...], wdt[tap * C:tap * C + C]).reshape(4, 4, T, C)
        back2[:, tap // 2, :, tap % 2] = back
    pad2[...] = jnp.zeros_like(pad2)
    slope_pad[...] = jnp.zeros_like(slope_pad)

    def fill_rims(n, pad):
        edges, corners = ex_wait(n)
        rims = mm(r_mat[...], edges).astype(BF16).reshape(4, S, T, C)
        cells = mm(rc_mat[...], corners).astype(BF16)
        pad[0, 1:9] = rims[0]
        pad[1:9, 9] = rims[1]
        pad[9, 1:9] = rims[2]
        pad[1:9, 0] = rims[3]
        pad[0, 9] = cells[0:16]
        pad[9, 9] = cells[16:32]
        pad[9, 0] = cells[32:48]
        pad[0, 0] = cells[48:64]

    def taps_sum(read, w):
        out = None
        for a in range(0, 9, 2):
            taps = TAPS[a:a + 2]
            lhs = [read(p, q) for p, q in taps]
            lhs = lhs[0] if len(lhs) == 1 else jnp.concatenate(lhs, axis=1)
            part = mm(lhs, w[a * C:(a + len(taps)) * C])
            out = part if out is None else out + part
        return out

    def conv(pad, w, i):
        return taps_sum(lambda p, q: pad[i + p:i + p + 2, q:q + 8].reshape(256, C), w)

    def logistic(v):
        return 1.0 / (1.0 + jnp.exp(-v))

    fill_rims(0, pad1)
    for i in range(0, S, 2):
        v = conv(pad1, w1_ref, i)
        pre1[i:i + 2] = v.reshape(2, S, T, C)
        pad2[1 + i:3 + i, 1:9] = (v * logistic(v)).astype(BF16).reshape(2, S, T, C)
    gather(1, pad2[1:9, 1:9].reshape(PIX, C))
    ex_start(1)
    fill_rims(1, pad2)
    for i in range(0, S, 2):
        v = conv(pad2, w2_ref, i)
        s = logistic(v)
        hid2[i // 2] = (v * s).astype(BF16).reshape(2, 4, 2, T, C)
        d = back2[i // 2].reshape(256, C) * (s * (1.0 + v * (1.0 - s)))
        slope_pad[2 + i:4 + i, 2:10] = d.astype(BF16).reshape(2, S, T, C)
        slope_t[:, i * 128:i * 128 + 256] = jnp.transpose(d).astype(BF16)

    def conv_back(wt):
        for a in range(0, 10, 2):
            v = taps_sum(
                lambda p, q: slope_pad[a + 2 - p:a + 4 - p, 2 - q:12 - q].reshape(320, C), wt
            )
            bp[a:a + 2] = v.reshape(2, 10, T, C)

    def return_rims(n):
        rims = [bp[0, 1:9], bp[1:9, 9], bp[9, 1:9], bp[1:9, 0]]
        edges = jnp.concatenate([r.astype(BF16).reshape(S * T, C) for r in rims], axis=0)
        cells = [bp[0, 9], bp[9, 9], bp[9, 0], bp[0, 0], jnp.zeros((64, C), F32)]
        corners = jnp.concatenate(cells, axis=0).astype(BF16)
        pack(n, mm(rt_mat[...], edges), mm(rct_mat[...], corners))
        ex_start(n)

    def returned(n):
        edges, corners = ex_wait(n)
        inner = bp[1:9, 1:9].reshape(PIX, C)
        return inner + mm(gt_mat[...], edges) + mm(gct_mat[...], corners)

    conv_back(w2t)
    return_rims(2)

    def hid_tap(p, q):
        return hid2[:, p, :, q].reshape(256, C)

    feats = None
    for tap in range(4):
        part = mm(hid_tap(tap // 2, tap % 2), wd_ref[tap * C:tap * C + C])
        feats = part if feats is None else feats + part
    small[...] = feats
    for t in range(T):
        feat_ref[pl.ds(t * 16, 16), :] = small[pl.ds(t, 16, stride=T), :].astype(BF16)

    def put(gf, tap, per_half, at, value):
        value = jnp.transpose(value).reshape(8, 16, C)
        low = tap * 8
        for half in range(2):
            lo, hi = max(low, half * per_half), min(low + 8, (half + 1) * per_half)
            if lo < hi:
                gf[half, at + lo - half * per_half:at + hi - half * per_half] = (
                    value[lo - low:hi - low]
                )

    for tap in range(4):
        put(gf0, tap, 16, 36, mm(cot_t[...], hid_tap(tap // 2, tap % 2)))

    def weight_grad(pad, gf):
        for a in range(0, 9, 2):
            taps = TAPS[a:a + 2]
            rhs = [pad[p:p + 8, q:q + 8].reshape(PIX, C) for p, q in taps]
            rhs = rhs[0] if len(rhs) == 1 else jnp.concatenate(rhs, axis=1)
            both = mm(slope_t[...], rhs)
            for j in range(len(taps)):
                put(gf, a + j, 36, 0, both[:, j * C:(j + 1) * C])

    weight_grad(pad2, gf0)

    late = ((gf0, s_a0, r_a0, r_c0), (gf1, s_a1, r_a1, r_c1))

    def swap(n):
        gf, s_a, r_a, _ = late[n]
        return pltpu.make_async_remote_copy(
            src_ref=s_a, dst_ref=r_a, send_sem=red_send.at[n, 0], recv_sem=red_recv.at[n, 0],
            device_id=(dp, me + 1 - 2 * core), device_id_type=MESH,
        )

    def swap_start(n):
        gf, s_a, r_a, _ = late[n]
        s_a[...] = (gf[1 - core] * GRAD_SCALE).astype(BF16)
        swap(n).start()

    def block_copy(n, b):
        return pltpu.make_async_remote_copy(
            src_ref=s_b.at[n, b], dst_ref=r_b.at[n, chip],
            send_sem=red_send.at[n, 1], recv_sem=red_recv.at[n, 1],
            device_id=(lax.div(b, 32), lax.rem(b, 32) * 2 + core), device_id_type=MESH,
        )

    def block_many(n, count):
        at = pl.ds(0, count)
        return pltpu.make_async_remote_copy(
            src_ref=s_b.at[n, at], dst_ref=r_b.at[n, at],
            send_sem=red_send.at[n, 1], recv_sem=red_recv.at[n, 1],
            device_id=(dp, me + 1 - 2 * core), device_id_type=MESH,
        )

    def scatter_start(n):
        gf, s_a, r_a, _ = late[n]
        nb = NB_LATE[n]
        swap(n).wait_recv()
        s_b[n, 0:nb] = (gf[core] * GRAD_SCALE + r_a[...].astype(F32)).astype(BF16)

        def send(o, carry):
            b = lax.rem(chip + o, 64)

            @pl.when(b < nb)
            def _():
                block_copy(n, b).start()

            return carry

        lax.fori_loop(1, 64, send, 0)

        @pl.when(chip < nb)
        def _():
            r_b[n, chip] = s_b[n, chip]

    def share_copy(n, t):
        return pltpu.make_async_remote_copy(
            src_ref=s_c.at[n], dst_ref=late[n][3].at[chip],
            send_sem=red_send.at[n, 2], recv_sem=red_recv.at[n, 2],
            device_id=(core, t), device_id_type=MESH,
        )

    def share_many(n, count):
        at = pl.ds(0, count)
        return pltpu.make_async_remote_copy(
            src_ref=r_b.at[n, at], dst_ref=r_b.at[n, at],
            send_sem=red_send.at[n, 2], recv_sem=red_recv.at[n, 2],
            device_id=(dp, me + 1 - 2 * core), device_id_type=MESH,
        )

    def share_start(n):
        nb = NB_LATE[n]

        @pl.when(chip < nb)
        def _():
            block_many(n, 63).wait_recv()
            total = jnp.sum(r_b[n].astype(F32), axis=0)
            s_c[n] = total.astype(BF16)

            def send(o, carry):
                share_copy(n, lax.rem(me + o, N_TILE)).start()
                return carry

            lax.fori_loop(1, N_TILE, send, 0)

            @pl.when(dp != core)
            def _():
                share_copy(n, me).start()

            @pl.when(dp == core)
            def _():
                late[n][3][chip] = s_c[n]

    def share_wait(n):
        nb = NB_LATE[n]
        mine = jnp.logical_and(chip < nb, dp == core)

        @pl.when(mine)
        def _():
            share_many(n, nb - 1).wait_recv()

        @pl.when(jnp.logical_not(mine))
        def _():
            share_many(n, nb).wait_recv()

    swap_start(0)

    scatter_start(0)
    grad = returned(2)
    for i in range(0, S, 2):
        v = pre1[i:i + 2].reshape(256, C)
        s = logistic(v)
        d = grad[i * 128:i * 128 + 256] * (s * (1.0 + v * (1.0 - s)))
        slope_pad[2 + i:4 + i, 2:10] = d.astype(BF16).reshape(2, S, T, C)
        slope_t[:, i * 128:i * 128 + 256] = jnp.transpose(d).astype(BF16)
    weight_grad(pad1, gf1)
    swap_start(1)
    conv_back(w1t)
    return_rims(3)
    scatter_start(1)
    share_start(0)
    wide[...] = returned(3)
    for t in range(T):
        ig_ref[pl.ds(t * 64, 64), :] = wide[pl.ds(t, 64, stride=T), :]
    share_start(1)
    share_wait(0)
    o2_ref[...] = r_c0[0:36].astype(F32).reshape(576, C)
    od_ref[...] = r_c0[36:52].astype(F32).reshape(256, C)
    share_wait(1)
    o1_ref[...] = r_c1[...].astype(F32).reshape(576, C)

    for n in range(4):
        e, c = ex_all(n)
        e.wait_send()
        c.wait_send()
    for n in range(2):
        nb = NB_LATE[n]
        swap(n).wait_send()

        @pl.when(chip < nb)
        def _():
            block_many(n, nb - 1).wait_send()

            @pl.when(dp == core)
            def _():
                share_many(n, 63).wait_send()

            @pl.when(dp != core)
            def _():
                share_many(n, 64).wait_send()

        @pl.when(chip >= nb)
        def _():
            block_many(n, nb).wait_send()


def local(inputs, cotangent, w_first, w_second, w_down, edge_owner, corner_owner, neighbour_tile, seam_rotation):
    vmem = pl.BlockSpec(memory_space=pltpu.VMEM)
    v = pltpu.VMEM
    outs = pl.pallas_call(
        kernel,
        out_shape=(
            jax.ShapeDtypeStruct((256, C), BF16),
            jax.ShapeDtypeStruct((1024, C), F32),
            jax.ShapeDtypeStruct((576, C), F32),
            jax.ShapeDtypeStruct((576, C), F32),
            jax.ShapeDtypeStruct((256, C), F32),
        ),
        in_specs=[vmem] * 9,
        out_specs=(vmem,) * 5,
        scratch_shapes=[
            v((1024, C), F32),
            v((10, 10, T, C), F32),
            v((S, S, T, C), F32),
            v((10, 10, T, C), BF16),
            v((10, 10, T, C), BF16),
            v((12, 12, T, C), BF16),
            v((1024, 1024), BF16),
            v((1024, 1024), BF16),
            v((128, 1024), BF16),
            v((1024, 128), BF16),
            v((512, 1024), BF16),
            v((1024, 512), BF16),
            v((128, 128), BF16),
            v((128, 128), BF16),
            v((1152, C), BF16),
            v((1152, C), BF16),
            v((512, C), BF16),
            v((4, 2, 4, 2, T, C), F32),
            v((4, 2, 4, 2, T, C), BF16),
            v((256, C), BF16),
            v((C, 256), BF16),
            v((C, 1024), BF16),
            v((256, C), F32),
            v((2, 52, 16, C), F32),
            v((2, 36, 16, C), F32),
            v((52, 16, C), BF16),
            v((36, 16, C), BF16),
            v((52, 16, C), BF16),
            v((36, 16, C), BF16),
            v((2, 64, 16, C), BF16),
            v((2, 64, 16, C), BF16),
            v((2, 16, C), BF16),
            v((52, 16, C), BF16),
            v((36, 16, C), BF16),
            v((4, N_TILE, T, C), BF16),
            v((4, N_TILE, T, C), BF16),
            v((4, N_TILE, 2, C), BF16),
            v((4, N_TILE, 2, C), BF16),
            pltpu.SemaphoreType.DMA((4, 2)),
            pltpu.SemaphoreType.DMA((4, 2)),
            pltpu.SemaphoreType.DMA((2, 3)),
            pltpu.SemaphoreType.DMA((2, 3)),
        ],
        compiler_params=pltpu.CompilerParams(
            collective_id=0, has_side_effects=True, vmem_limit_bytes=60 * 1024 * 1024
        ),
    )(
        inputs.reshape(1024, C), cotangent.reshape(256, C), w_first, w_second, w_down,
        edge_owner.T, corner_owner.T, neighbour_tile.T, seam_rotation.T,
    )
    feats, grads, one, two, low = outs
    return (feats.reshape(1, T, 4, 4, C), grads.reshape(1, T, S, S, C), one, two, low)


def solution(mesh):
    tiles = P("dp", "tile", None, None, None)
    return jax.shard_map(
        local,
        mesh=mesh,
        in_specs=(tiles, tiles) + (P(),) * 7,
        out_specs=(tiles, tiles) + (P("dp", None),) * 3,
        check_vma=False,
    )
```

time: 579 us -> 68.1 us (0.12); the launches traced: 570 us -> 67.8 us
  blocking collectives: 289 us -> 0 us
  local copies, waits for them, and re-layouts: 99.7 us -> 6.16 us
  Pallas kernels: 0 us -> 61 us
  starting transfers between devices: 53.7 us -> 0 us
  other arithmetic: 38.7 us -> 0 us
  waiting for transfers between devices: 38.6 us -> 0 us
  matrix products: 34.1 us -> 0 us
  between operations: 16 us -> 0.65 us
    psum x1 -> x0, blocking collectives: 289 us -> none  [local(): summed = lax.psum((grad_one, grad_two, grad_low), 'tile')]
    pallas_call x0 -> x1, Pallas kernels: none -> 61 us  [local(): pl.pallas_call(kernel, out_shape=(jax.ShapeDtypeStruct((256, C), BF16), j...]
    all_to_all x8 -> x0, starting transfers between devices: 53.4 us -> none  [the longest x2 15.4 us: return_rims(): lax.all_to_all(edge_back.astype(jnp.bfloat16), 'tile', split_axis=0, conc...]
    scatter-add x14 -> x0, local copies, waits for them, and re-layouts: 43.8 us -> none  [conv_adjoint(): back_pad = back_pad.at[:, row_off:row_off + out_rows, col_off:col_off + o...]
    all_to_all x8 -> x0, waiting for transfers between devices: 38 us -> none  [the longest x2 17.3 us: fetch_rims(): lax.all_to_all(edge_vals, 'tile', split_axis=0, concat_axis=0, tiled=True)]
    dot_general x66 -> x0, matrix products: 34.1 us -> none  [the longest x18 15 us: conv_adjoint(): lax.dot_general(slope_rows, weight[tap_start:tap_start + channels], (((1,...]
    gather x36 -> x0, local copies, waits for them, and re-layouts: 28.7 us -> none  [the longest x2 11.7 us: fetch_rims(): edge_vals = tile_pixels[edge_src[:, :, None], edge_pix]]
    scatter-add x4 -> x0, other arithmetic: 16 us -> none  [the longest x2 12.8 us: return_rims(): interior = interior.at[edge_index].add(got_edges.reshape(-1, channels))]
  transfers between devices with their start and end apart: 11 -> 0, of which waited for: 6 -> 0; matrix products, arithmetic and copies ran while one was open for 14% -> 0% of each run, Pallas kernels for 0% -> 0%
where the time goes in v1:
time: 68.1 us; the launch traced here: 67.8 us
  Pallas kernels  61 us (90%)
  local copies, waits for them, and re-layouts  6.16 us (9%)
    pallas_call x1, Pallas kernels, local(): pl.pallas_call(kernel, out_shape=(jax.ShapeDtypeStruct((256, C), BF16), j...  61 us
    unnamed x11, local copies, waits for them, and re-layouts  6.16 us

profile of v1, /device:TPU:1, one launch (start us, length us, event | category | flops | bytes accessed | tf_op | source)
XLA Modules:
  0.0 67.8 jit_solution(7629624972899765498)
XLA Ops:
  0.6 61.0 %shard_map.128 = (bf16[256,128]{1,0:T(8,128)(2,1)}, f32[1024,128]{1,0:T(8,128)}, f32[576,128]{1,0:T(8,128)}, f32[576,128]{1,0:T(8,128)}, f32[256,128]{1,0:T(8,128)}) custom-call(bf16[1024,128]{1,0:T(8,128)(2,1)} %bitcast.9, bf16[256,128]{1,0:T(8,128)(2,1)} %bitcast.10, bf16[1152,128]{1,0:T(8,128)(2,1)} %w1_ref.1, bf16[1152,128]{1,0:T(8,128)(2,1)} %w2_ref.1, ...), custom_call_target="tpu_custom_call" | custom-call | tf_op jit(solution)/shard_map/pallas_call | solution.py:513
  61.7 1.5 %copy.19 = bf16[1,16,4,4,128]{4,3,2,1,0:T(4,128)(2,1)} copy(bf16[1,16,4,4,128]{4,3,2,1,0:T(4,128)(2,1)} %bitcast.11) | data formatting | bytes 131072
  63.1 0.0 copy-start.1
  63.2 1.9 %copy.20 = f32[1,16,8,8,128]{4,3,2,1,0:T(8,128)} copy(f32[1,16,8,8,128]{4,3,2,1,0:T(8,128)} %bitcast.8) | data formatting | bytes 1048576
  65.1 0.0 copy-done.1
  65.1 0.0 copy-start
  65.1 0.7 %copy.21 = f32[576,128]{1,0:T(8,128)} copy(f32[576,128]{1,0:T(8,128)S(1)} %copy-done.1) | data formatting | bytes 589824
  65.8 0.4 copy-done
  66.2 0.0 copy-start.2
  66.2 0.7 %copy.22 = f32[576,128]{1,0:T(8,128)} copy(f32[576,128]{1,0:T(8,128)S(1)} %copy-done) | data formatting | bytes 589824
  66.9 0.3 copy-done.2
  67.2 0.7 copy.23
Async XLA Ops:
  63.1 1.9 %copy-start.1 = (f32[576,128]{1,0:T(8,128)S(1)}, f32[576,128]{1,0:T(8,128)}, u32[]{:S(2)}) copy-start(f32[576,128]{1,0:T(8,128)} %get-tuple-element.22) | copy-start | bytes 884740
  65.1 1.1 %copy-start = (f32[576,128]{1,0:T(8,128)S(1)}, f32[576,128]{1,0:T(8,128)}, u32[]{:S(2)}) copy-start(f32[576,128]{1,0:T(8,128)} %get-tuple-element.23) | copy-start | bytes 884740
  66.2 1.0 %copy-start.2 = (f32[256,128]{1,0:T(8,128)S(1)}, f32[256,128]{1,0:T(8,128)}, u32[]{:S(2)}) copy-start(f32[256,128]{1,0:T(8,128)} %get-tuple-element.24) | copy-start | bytes 393220

commit v2 on v1

v2 whole, which is shorter than its diff:
```python
import itertools

import jax
import jax.numpy as jnp
import numpy as np
from jax import lax
from jax.experimental import pallas as pl
from jax.experimental.pallas import tpu as pltpu
from jax.sharding import PartitionSpec as P

MESH = pl.DeviceIdType.MESH
F32 = jnp.float32
BF16 = jnp.bfloat16
N_TILE = 64
T = 16
S = 8
C = 128
PIX = S * S * T
TAPS = [(p, q) for p in range(3) for q in range(3)]
GRAD_SCALE = float(2 * 1024 * 64) ** -0.5
BLOCKS = (36 + 16, 36)


def hops(rel):
    return min(rel[0], 4 - rel[0]) + rel[1] + min(rel[2], 4 - rel[2]) + 0.3 * rel[3]


OFFSETS = sorted(itertools.product(range(4), range(2), range(4), range(2)), key=hops, reverse=True)
PEERS = OFFSETS[:-1]
EDGE_LINES = [(0, slice(0, 8)), (7, slice(0, 8)), (slice(1, 7), 0), (slice(1, 7), 7)]
INSIDE = (slice(1, 7), slice(1, 7))


def seam_lines():
    grid = np.arange(S * S).reshape(S, S)
    sides = [grid[0], grid[-1], grid[:, 0], grid[:, -1]]
    first = np.zeros((8, 4), int)
    step = np.zeros((8, 4), int)
    for turn in range(4):
        turned = np.rot90(grid, turn)
        lines = [turned[-1, :], turned[:, 0], turned[0, :], turned[:, -1]]
        for k, line in enumerate(lines):
            for n, side in enumerate(sides):
                if (line == side).all():
                    first[k, turn], step[k, turn] = 8 * n, 1
                if (line[::-1] == side).all():
                    first[k, turn], step[k, turn] = 8 * n + 7, -1
        cells = [turned[-1, 0], turned[0, 0], turned[0, -1], turned[-1, -1]]
        for k, cell in enumerate(cells):
            first[4 + k, turn] = {0: 0, 7: 7, 56: 8, 63: 15}[int(cell)]
    return first, step


def iota(shape, axis):
    return lax.broadcasted_iota(jnp.int32, shape, axis)


def hot(mask):
    return jnp.where(mask, 1.0, 0.0).astype(BF16)


def mm(a, b):
    return jnp.dot(a, b, preferred_element_type=F32)


def mm_nt(a, b):
    return lax.dot_general(a, b, (((1,), (1,)), ((), ())), preferred_element_type=F32)


def logistic(v):
    return 1.0 / (1.0 + jnp.exp(-v))


def silu_slope(v):
    s = logistic(v)
    return s * (1.0 + v * (1.0 - s))


def flip(w):
    return jnp.transpose(w.astype(F32)).astype(BF16)


def flat(v):
    return v.reshape(-1, C)


def cells(v):
    return v.reshape(-1, T, C)


def moved(region, by):
    return tuple(slice(r.start + by, r.stop + by) if isinstance(r, slice) else r + by for r in region)


def kernel(
    x_hbm, cot_hbm, w1_hbm, w2_hbm, wd_hbm, eo_hbm, co_hbm, nb_hbm, rot_hbm,
    feat_ref, ig_ref, late0_ref, late1_ref,
    x_ref, cot_ref, w1_ref, w2_ref, wd_ref, eo_ref, co_ref, nb_ref, rot_ref,
    wide, inner, pre1, pre2, pad1, pad2, slope_pad, g_mat, gt_mat, gc_mat, gct_mat,
    r_mat, rt_mat, rc_mat, rct_mat, w1t, w2t, wdt, back6, back2, hid2, cot_p, cot_t,
    small, gf0, gf1, s_a0, s_a1, r_a0, r_a1, s_b, r_b, s_c, r_c0, r_c1,
    s_edge, r_edge, s_corner, r_corner,
    load_sem, ex_send, ex_recv, red_send, red_recv,
):
    dp = lax.axis_index("dp")
    me = lax.axis_index("tile")
    core = lax.rem(me, 2)
    chip = dp * 32 + lax.div(me, 2)
    at_x = [lax.rem(lax.div(me, 16) + d, 4) * 16 for d in range(4)]
    at_z = [lax.rem(lax.div(me, 8) + d, 2) * 8 for d in range(2)]
    at_y = [lax.rem(lax.div(me, 2) + d, 4) * 2 for d in range(4)]
    at_c = [lax.rem(me + d, 2) for d in range(2)]

    def peer(rel):
        return at_x[rel[0]] + at_z[rel[1]] + at_y[rel[2]] + at_c[rel[3]]

    pairs = [
        (eo_hbm, eo_ref), (co_hbm, co_ref), (nb_hbm, nb_ref), (rot_hbm, rot_ref), (x_hbm, x_ref),
        (cot_hbm, cot_ref), (w1_hbm, w1_ref), (w2_hbm, w2_ref), (wd_hbm, wd_ref),
    ]
    loads = [pltpu.make_async_copy(a, b, load_sem.at[i]) for i, (a, b) in enumerate(pairs)]
    for load in loads:
        load.start()
    barrier = pltpu.get_barrier_semaphore()
    pl.semaphore_signal(barrier, inc=1, device_id=(1 - dp, me), device_id_type=MESH)
    for rel in PEERS:
        pl.semaphore_signal(barrier, inc=1, device_id=(dp, peer(rel)), device_id_type=MESH)
    for load in loads[:4]:
        load.wait()

    me_f = me.astype(F32)
    own = jnp.concatenate([eo_ref[...], co_ref[...]], axis=0).astype(F32)
    src = nb_ref[...].astype(F32)
    rot = rot_ref[...].astype(F32)
    row8 = iota((8, 1024), 0)
    first, step = seam_lines()
    base_v = jnp.zeros((8, 1024), F32)
    step_v = jnp.zeros((8, 1024), F32)
    for turn in range(4):
        bcol = jnp.zeros((8, 1024), F32)
        scol = jnp.zeros((8, 1024), F32)
        for k in range(8):
            bcol = jnp.where(row8 == k, float(first[k, turn]), bcol)
            scol = jnp.where(row8 == k, float(step[k, turn]), scol)
        base_v = jnp.where(rot == float(turn), bcol, base_v)
        step_v = jnp.where(rot == float(turn), scol, step_v)
    match = jnp.where(own == me_f, 1.0, 0.0)

    def per_kind(v):
        a = jnp.broadcast_to(jnp.sum(v[0:4], axis=0, keepdims=True), (4, 1024))
        b = jnp.broadcast_to(jnp.sum(v[4:8], axis=0, keepdims=True), (4, 1024))
        return jnp.concatenate([a, b], axis=0)

    has = per_kind(match)
    lane16 = jnp.bitwise_and(iota((8, 1024), 1), 15)
    acc = has
    for sh in (1, 2, 4, 8):
        acc = acc + jnp.where(lane16 >= sh, pltpu.roll(acc, sh, 1), 0.0)
    rank = acc - has
    table = []
    for s in range(2):
        sel = match * jnp.where(rank == float(s), 1.0, 0.0)
        for v in (sel, sel * base_v, sel * step_v, sel * src):
            table.append(per_kind(v))
    tab = jnp.concatenate([v[0:1] for v in table] + [v[4:5] for v in table], axis=0).astype(BF16)
    lane_i = iota((1, 1024), 1)
    sub_i = iota((1024, 1), 0)
    lane_f = lane_i.astype(F32)
    sub_f = sub_i.astype(F32)
    blk_l = jnp.right_shift(lane_i, 4).astype(F32)
    blk_s = jnp.right_shift(sub_i, 4).astype(F32)
    block_diag = hot(blk_s == blk_l)
    slots_e = mm(tab, block_diag)
    pair_s = jnp.right_shift(iota((128, 1), 0), 1).astype(F32)
    slots_c = mm_nt(tab, hot(pair_s == blk_l))

    def target(rows, which, px):
        v0, b0, t0, n0, v1, b1, t1, n1 = [rows[i:i + 1] for i in range(8)]
        late = which > 0.5
        valid = jnp.where(late, v1, v0)
        line = jnp.where(late, b1, b0) + jnp.where(late, t1, t0) * px
        return jnp.where(valid > 0.5, line * float(T) + jnp.where(late, n1, n0), -1.0)

    te = target(
        slots_e[0:8],
        jnp.bitwise_and(jnp.right_shift(lane_i, 3), 1).astype(F32),
        jnp.bitwise_and(lane_i, 7).astype(F32),
    )
    tc = target(slots_c[8:16], jnp.bitwise_and(lane_i[:, :128], 1).astype(F32), 0.0)

    def as_column(row, n):
        return jnp.transpose(jnp.broadcast_to(row, (128, n)))[:, 0:1]

    g_mat[...] = hot(as_column(te, 1024) == lane_f[:, :512])
    gc_mat[...] = hot(as_column(tc, 128) == lane_f[:, :512])

    pad1[...] = jnp.zeros_like(pad1)
    loads[4].wait()
    wide[...] = x_ref[...].astype(F32)
    for px in range(S * S):
        pad1[1 + px // S, 1 + px % S] = wide[pl.ds(px, T, stride=S * S), :].astype(BF16)

    def pack(n, edges, corners):
        s_edge[n] = edges.astype(BF16).reshape(N_TILE, T, C)
        s_corner[n] = corners.astype(BF16).reshape(N_TILE, 2, C)

    def gather(n, pad):
        lines = [pad[1, 1:9], pad[8, 1:9], pad[1:9, 1], pad[1:9, 8]]
        lines = jnp.concatenate([flat(v) for v in lines], axis=0)
        pack(n, mm(g_mat[...], lines), mm(gc_mat[...], lines))

    def ex_copies(n, src_at, dst_at, d):
        e = pltpu.make_async_remote_copy(
            src_ref=s_edge.at[n, src_at], dst_ref=r_edge.at[n, dst_at],
            send_sem=ex_send.at[n, 0], recv_sem=ex_recv.at[n, 0],
            device_id=(dp, d), device_id_type=MESH,
        )
        c = pltpu.make_async_remote_copy(
            src_ref=s_corner.at[n, src_at], dst_ref=r_corner.at[n, dst_at],
            send_sem=ex_send.at[n, 1], recv_sem=ex_recv.at[n, 1],
            device_id=(dp, d), device_id_type=MESH,
        )
        return e, c

    def ex_start(n):
        for rel in PEERS:
            d = peer(rel)
            for copy in ex_copies(n, d, me, d):
                copy.start()
        r_edge[n, me] = s_edge[n, me]
        r_corner[n, me] = s_corner[n, me]

    def ex_all(n):
        rest = pl.ds(0, N_TILE - 1)
        return ex_copies(n, rest, rest, peer(OFFSETS[0]))

    def ex_wait(n):
        for copy in ex_all(n):
            copy.wait_recv()
        return flat(r_edge[n]), flat(r_corner[n])

    gather(0, pad1)
    pl.semaphore_wait(barrier, N_TILE)
    ex_start(0)

    for load in loads[5:]:
        load.wait()
    ownb = own.astype(BF16)
    pick = hot(iota((128, 1), 0).astype(F32) + me_f * float(T) == lane_f)
    my_row = mm_nt(ownb, pick)
    my_col = mm_nt(pick[0:16], ownb)
    earlier = iota((T, 128), 1).astype(F32) < iota((T, 128), 0).astype(F32)

    def slot_base(kind, per_owner, per_rank):
        out = []
        for k in range(4 * kind, 4 * kind + 4):
            col = my_col[:, k:k + 1]
            shared = jnp.zeros((T, 128), F32)
            for k2 in range(4 * kind, 4 * kind + 4):
                shared = shared + jnp.where(col == my_row[k2:k2 + 1], 1.0, 0.0)
            rk = jnp.sum(jnp.where(earlier, shared, 0.0), axis=1, keepdims=True)
            out.append(col * per_owner + rk * per_rank)
        return out

    base_e = slot_base(0, 16.0, 8.0)
    base_c = slot_base(1, 2.0, 1.0)
    col_e = jnp.concatenate([b + float(px) for b in base_e for px in range(S)], axis=0)
    col_c = jnp.concatenate(base_c + [jnp.full((64, 1), -1.0, F32)], axis=0)
    r_mat[...] = hot(col_e == lane_f)
    rc_mat[...] = hot(col_c == lane_f[:, :128])

    def taps_sum(read, w):
        out = None
        for a in range(0, 9, 2):
            taps = TAPS[a:a + 2]
            lhs = [read(p, q) for p, q in taps]
            lhs = lhs[0] if len(lhs) == 1 else jnp.concatenate(lhs, axis=1)
            part = mm(lhs, w[a * C:(a + len(taps)) * C])
            out = part if out is None else out + part
        return out

    def conv_centre(pad, w, pre):
        for i in range(0, S, 2):
            v = taps_sum(lambda p, q: flat(pad[i + p:i + p + 2, q:q + 8]), w)
            pre[i:i + 2] = v.reshape(2, S, T, C)

    def first_act(region):
        v = pre1[region]
        pad2[moved(region, 1)] = (v * logistic(v)).astype(BF16)

    pad2[...] = jnp.zeros_like(pad2)
    slope_pad[...] = jnp.zeros_like(slope_pad)
    conv_centre(pad1, w1_ref, pre1)
    first_act(INSIDE)
    for tap in range(4):
        at = slice(tap * C, tap * C + C)
        wdt[at] = flip(wd_ref[at])
    small[...] = cot_ref[...].astype(F32)
    for px in range(16):
        cot_p[pl.ds(px * T, T), :] = small[pl.ds(px, T, stride=16), :].astype(BF16)
    for tap in range(4):
        back = mm(cot_p[...], wdt[tap * C:tap * C + C]).reshape(4, 4, T, C)
        back6[:, tap // 2, :, tap % 2] = back
    back2[...] = back6[...].reshape(S, S, T, C)
    for tap in range(9):
        at = slice(tap * C, tap * C + C)
        w2t[at] = flip(w2_ref[at])

    def fill_rims(n, pad):
        edges, corners = ex_wait(n)
        rims = mm(r_mat[...], edges).astype(BF16).reshape(4, S, T, C)
        at_corner = mm(rc_mat[...], corners).astype(BF16)
        pad[0, 1:9] = rims[0]
        pad[1:9, 9] = rims[1]
        pad[9, 1:9] = rims[2]
        pad[1:9, 0] = rims[3]
        pad[0, 9] = at_corner[0:16]
        pad[9, 9] = at_corner[16:32]
        pad[9, 0] = at_corner[32:48]
        pad[0, 0] = at_corner[48:64]

    def rim_taps(pad, w, pre):
        for i, row, p in ((0, 0, 0), (7, 9, 2)):
            lhs = jnp.concatenate([flat(pad[row, q:q + 8]) for q in range(3)], axis=1)
            pre[i] = pre[i] + cells(mm(lhs, w[3 * p * C:(3 * p + 3) * C]))
        zero = jnp.zeros((T, C), BF16)
        for j, col, q in ((0, 0, 0), (7, 9, 2)):
            lhs = [
                jnp.concatenate([zero, flat(pad[1:8, col])], axis=0),
                flat(pad[1:9, col]),
                jnp.concatenate([flat(pad[2:9, col]), zero], axis=0),
            ]
            part = None
            for p in range(3):
                one = mm(lhs[p], w[(3 * p + q) * C:(3 * p + q + 1) * C])
                part = one if part is None else part + one
            pre[:, j] = pre[:, j] + cells(part)

    fill_rims(0, pad1)
    rim_taps(pad1, w1_ref, pre1)
    for region in EDGE_LINES:
        first_act(region)
    gather(1, pad2)
    ex_start(1)

    conv_centre(pad2, w2_ref, pre2)

    def second_act(region):
        v = pre2[region]
        s = logistic(v)
        hid2[region] = (v * s).astype(BF16)
        slope_pad[moved(region, 2)] = (back2[region] * (s * (1.0 + v * (1.0 - s)))).astype(BF16)

    second_act(INSIDE)
    cot_t[...] = flip(cot_p[...])
    for tap in range(9):
        at = slice(tap * C, tap * C + C)
        w1t[at] = flip(w1_ref[at])
    row_e = jnp.transpose(jnp.broadcast_to(col_e, (512, 128)))[0:1]
    row_c = jnp.transpose(jnp.broadcast_to(col_c, (128, 128)))[0:1]
    rt_mat[...] = hot(sub_f == row_e)
    rct_mat[...] = hot(sub_f[:128] == row_c)
    gt_mat[...] = hot(sub_f[:512] == te)
    gct_mat[...] = hot(sub_f[:512] == tc)

    def return_rims(n, wt):
        rows = []
        for row, p in ((2, 0), (9, 2)):
            lhs = jnp.concatenate([flat(slope_pad[row, 2 - q:12 - q]) for q in range(3)], axis=1)
            rows.append(mm(lhs, wt[3 * p * C:(3 * p + 3) * C]).astype(BF16))
        cols = []
        for col, q in ((2, 0), (9, 2)):
            part = None
            for p in range(3):
                at = slice((3 * p + q) * C, (3 * p + q + 1) * C)
                one = mm(flat(slope_pad[3 - p:11 - p, col]), wt[at])
                part = one if part is None else part + one
            cols.append(part.astype(BF16))
        top, bottom = rows
        left, right = cols
        edges = jnp.concatenate([top[T:9 * T], right, bottom[T:9 * T], left], axis=0)
        corners = jnp.concatenate(
            [top[9 * T:], bottom[9 * T:], bottom[:T], top[:T], jnp.zeros((64, C), BF16)], axis=0
        )
        pack(n, mm(rt_mat[...], edges), mm(rct_mat[...], corners))
        ex_start(n)

    def back_centre(wt):
        for a in range(1, 9, 2):
            v = taps_sum(lambda p, q: flat(slope_pad[a + 2 - p:a + 4 - p, 3 - q:11 - q]), wt)
            inner[a - 1:a + 1] = v.reshape(2, S, T, C)

    def add_returned(n):
        edges, corners = ex_wait(n)
        lines = mm(gt_mat[...], edges) + mm(gct_mat[...], corners)
        lines = lines.reshape(4, S, T, C)
        inner[0] = inner[0] + lines[0]
        inner[7] = inner[7] + lines[1]
        inner[:, 0] = inner[:, 0] + lines[2]
        inner[:, 7] = inner[:, 7] + lines[3]

    fill_rims(1, pad2)
    rim_taps(pad2, w2_ref, pre2)
    for region in EDGE_LINES:
        second_act(region)
    return_rims(2, w2t)

    hid = hid2[...].reshape(4, 2, 4, 2, T, C)

    def hid_tap(tap):
        return flat(hid[:, tap // 2, :, tap % 2])

    def put(gf, tap, per_half, at, value, add=False):
        value = jnp.transpose(value).reshape(8, 16, C)
        low = tap * 8
        for half in range(2):
            lo, hi = max(low, half * per_half), min(low + 8, (half + 1) * per_half)
            if lo < hi:
                to = slice(at + lo - half * per_half, at + hi - half * per_half)
                part = value[lo - low:hi - low]
                gf[half, to] = gf[half, to] + part if add else part

    def weight_grad(slope_rows, read, gf, add=False):
        slope_t = flip(slope_rows)
        for a in range(0, 9, 2):
            taps = TAPS[a:a + 2]
            rhs = [read(p, q) for p, q in taps]
            rhs = rhs[0] if len(rhs) == 1 else jnp.concatenate(rhs, axis=1)
            both = mm(slope_t, rhs)
            for j in range(len(taps)):
                put(gf, a + j, 36, 0, both[:, j * C:(j + 1) * C], add)

    for tap in range(4):
        put(gf0, tap, 16, 36, mm(cot_t[...], hid_tap(tap)))
    weight_grad(
        flat(slope_pad[2:10, 2:10]), lambda p, q: flat(pad2[p:p + 8, q:q + 8]), gf0
    )

    late = ((gf0, s_a0, r_a0, r_c0), (gf1, s_a1, r_a1, r_c1))

    def owned(n, tile):
        nb = BLOCKS[n]
        b = lax.div(tile * nb + N_TILE - 1, N_TILE)
        return b, lax.div(b * N_TILE, nb) == tile

    def to_other_core(n, src_ref, dst_ref, stage):
        return pltpu.make_async_remote_copy(
            src_ref=src_ref, dst_ref=dst_ref,
            send_sem=red_send.at[n, stage], recv_sem=red_recv.at[n, stage],
            device_id=(dp, me + 1 - 2 * core), device_id_type=MESH,
        )

    def many(n, stage, count):
        at = pl.ds(0, count)
        return to_other_core(n, s_b.at[n, at], r_b.at[n, at], stage)

    def swap(n):
        return to_other_core(n, late[n][1], late[n][2], 0)

    def swap_start(n):
        gf, s_a = late[n][:2]
        s_a[...] = (gf[1 - core] * GRAD_SCALE).astype(BF16)
        swap(n).start()

    def scatter_start(n):
        gf, _, r_a, _ = late[n]
        swap(n).wait_recv()
        s_b[n, 0:BLOCKS[n]] = (gf[core] * GRAD_SCALE + r_a[...].astype(F32)).astype(BF16)
        for rel in OFFSETS:
            tile = peer(rel)
            b, owns = owned(n, tile)
            if rel == (0, 0, 0, 0):
                @pl.when(jnp.logical_and(owns, dp == core))
                def _():
                    r_b[n, chip] = s_b[n, b]

                owns = jnp.logical_and(owns, dp != core)

            @pl.when(owns)
            def _():
                pltpu.make_async_remote_copy(
                    src_ref=s_b.at[n, b], dst_ref=r_b.at[n, chip],
                    send_sem=red_send.at[n, 1], recv_sem=red_recv.at[n, 1],
                    device_id=(core, tile), device_id_type=MESH,
                ).start()

    def share_start(n):
        b, owns = owned(n, me)

        @pl.when(owns)
        def _():
            @pl.when(dp == core)
            def _():
                many(n, 1, 63).wait_recv()

            @pl.when(dp != core)
            def _():
                many(n, 1, 64).wait_recv()

            s_c[n] = jnp.sum(r_b[n].astype(F32), axis=0).astype(BF16)
            for rel in PEERS:
                pltpu.make_async_remote_copy(
                    src_ref=s_c.at[n], dst_ref=late[n][3].at[b],
                    send_sem=red_send.at[n, 2], recv_sem=red_recv.at[n, 2],
                    device_id=(dp, peer(rel)), device_id_type=MESH,
                ).start()
            late[n][3][b] = s_c[n]

    def share_wait(n):
        b, owns = owned(n, me)

        @pl.when(owns)
        def _():
            many(n, 2, BLOCKS[n] - 1).wait_recv()

        @pl.when(jnp.logical_not(owns))
        def _():
            many(n, 2, BLOCKS[n]).wait_recv()

    swap_start(0)
    back_centre(w2t)
    scatter_start(0)
    feats = None
    for tap in range(4):
        part = mm(hid_tap(tap), wd_ref[tap * C:tap * C + C])
        feats = part if feats is None else feats + part
    feat_ref[...] = feats

    def first_slope(region):
        slope_pad[moved(region, 2)] = (inner[region] * silu_slope(pre1[region])).astype(BF16)

    first_slope(INSIDE)
    weight_grad(
        flat(slope_pad[3:9, 3:9]), lambda p, q: flat(pad1[1 + p:7 + p, 1 + q:7 + q]), gf1
    )

    def edge_cells(ref, p, q):
        lines = [ref[p, q:q + 8], ref[7 + p, q:q + 8], ref[1 + p:7 + p, q], ref[1 + p:7 + p, 7 + q]]
        return jnp.concatenate([flat(v) for v in lines], axis=0)

    add_returned(2)
    for region in EDGE_LINES:
        first_slope(region)
    weight_grad(edge_cells(slope_pad, 2, 2), lambda p, q: edge_cells(pad1, p, q), gf1, add=True)
    swap_start(1)
    return_rims(3, w1t)
    scatter_start(1)
    share_start(0)
    back_centre(w1t)
    share_start(1)
    add_returned(3)
    ig_ref[...] = flat(inner[...])
    share_wait(0)
    late0_ref[...] = r_c0[...]
    share_wait(1)
    late1_ref[...] = r_c1[...]

    for n in range(4):
        for copy in ex_all(n):
            copy.wait_send()
    for n in range(2):
        nb = BLOCKS[n]
        swap(n).wait_send()
        b, owns = owned(n, me)
        kept = jnp.logical_and(owns, dp == core)

        @pl.when(kept)
        def _():
            many(n, 1, nb - 1).wait_send()

        @pl.when(jnp.logical_not(kept))
        def _():
            many(n, 1, nb).wait_send()

        @pl.when(owns)
        def _():
            many(n, 2, N_TILE - 1).wait_send()


def finish(feat_in, ig_in, late0, late1, feat_ref, ig_ref, o1_ref, o2_ref, od_ref):
    for t in range(T):
        feat_ref[pl.ds(t * 16, 16), :] = feat_in[pl.ds(t, 16, stride=T), :].astype(BF16)
        ig_ref[pl.ds(t * 64, 64), :] = ig_in[pl.ds(t, 64, stride=T), :]
    o1_ref[...] = flat(late1[...].astype(F32))
    o2_ref[...] = flat(late0[0:36].astype(F32))
    od_ref[...] = flat(late0[36:52].astype(F32))


def local(inputs, cotangent, w_first, w_second, w_down, edge_owner, corner_owner, neighbour_tile, seam_rotation):
    vmem = pl.BlockSpec(memory_space=pltpu.VMEM)
    v = pltpu.VMEM
    shape = jax.ShapeDtypeStruct
    between = pl.pallas_call(
        kernel,
        out_shape=(
            shape((256, C), F32), shape((1024, C), F32), shape((52, 16, C), BF16), shape((36, 16, C), BF16),
        ),
        in_specs=[pl.BlockSpec(memory_space=pltpu.HBM)] * 9,
        out_specs=(vmem,) * 4,
        scratch_shapes=[
            v((1024, C), BF16),
            v((256, C), BF16),
            v((1152, C), BF16),
            v((1152, C), BF16),
            v((512, C), BF16),
            v((4, 1024), jnp.int32),
            v((4, 1024), jnp.int32),
            v((8, 1024), jnp.int32),
            v((8, 1024), jnp.int32),
            v((1024, C), F32),
            v((S, S, T, C), F32),
            v((S, S, T, C), F32),
            v((S, S, T, C), F32),
            v((10, 10, T, C), BF16),
            v((10, 10, T, C), BF16),
            v((12, 12, T, C), BF16),
            v((1024, 512), BF16),
            v((512, 1024), BF16),
            v((128, 512), BF16),
            v((512, 128), BF16),
            v((512, 1024), BF16),
            v((1024, 512), BF16),
            v((128, 128), BF16),
            v((128, 128), BF16),
            v((1152, C), BF16),
            v((1152, C), BF16),
            v((512, C), BF16),
            v((4, 2, 4, 2, T, C), F32),
            v((S, S, T, C), F32),
            v((S, S, T, C), BF16),
            v((256, C), BF16),
            v((C, 256), BF16),
            v((256, C), F32),
            v((2, 52, 16, C), F32),
            v((2, 36, 16, C), F32),
            v((52, 16, C), BF16),
            v((36, 16, C), BF16),
            v((52, 16, C), BF16),
            v((36, 16, C), BF16),
            v((2, 64, 16, C), BF16),
            v((2, 64, 16, C), BF16),
            v((2, 16, C), BF16),
            v((52, 16, C), BF16),
            v((36, 16, C), BF16),
            v((4, N_TILE, T, C), BF16),
            v((4, N_TILE, T, C), BF16),
            v((4, N_TILE, 2, C), BF16),
            v((4, N_TILE, 2, C), BF16),
            pltpu.SemaphoreType.DMA((9,)),
            pltpu.SemaphoreType.DMA((4, 2)),
            pltpu.SemaphoreType.DMA((4, 2)),
            pltpu.SemaphoreType.DMA((2, 3)),
            pltpu.SemaphoreType.DMA((2, 3)),
        ],
        compiler_params=pltpu.CompilerParams(
            collective_id=0, has_side_effects=True, vmem_limit_bytes=32 * 1024 * 1024
        ),
    )(
        *[
            pltpu.with_memory_space_constraint(a, pltpu.HBM)
            for a in (
                inputs.reshape(1024, C), cotangent.reshape(256, C), w_first, w_second, w_down,
                edge_owner.T, corner_owner.T, neighbour_tile.T, seam_rotation.T,
            )
        ]
    )
    feats, grads, one, two, low = pl.pallas_call(
        finish,
        out_shape=(
            shape((256, C), BF16), shape((1024, C), F32), shape((576, C), F32),
            shape((576, C), F32), shape((256, C), F32),
        ),
        in_specs=[vmem] * 4,
        out_specs=(vmem,) * 5,
        compiler_params=pltpu.CompilerParams(vmem_limit_bytes=16 * 1024 * 1024),
    )(*between)
    return (feats.reshape(1, T, 4, 4, C), grads.reshape(1, T, S, S, C), one, two, low)


def solution(mesh):
    tiles = P("dp", "tile", None, None, None)
    return jax.shard_map(
        local,
        mesh=mesh,
        in_specs=(tiles, tiles) + (P(),) * 7,
        out_specs=(tiles, tiles) + (P("dp", None),) * 3,
        check_vma=False,
    )
```

time: 68.1 us -> 52.4 us (0.77)
  Pallas kernels: 61 us -> 51.6 us
  local copies, waits for them, and re-layouts: 6.16 us -> 0 us
    pallas_call x1 -> x2, Pallas kernels: 61 us -> 51.6 us  [the longest x1 50.4 us: local(): pl.pallas_call(kernel, out_shape=(shape((256, C), F32), shape((1024, C),...]
    unnamed x11 -> x0, local copies, waits for them, and re-layouts: 6.16 us -> none
where the time goes in v2:
time: 52.4 us; the launch traced here: 52.3 us
  Pallas kernels  51.6 us (98%)
  between operations  0.64 us (1%)
    pallas_call x1, Pallas kernels, local(): pl.pallas_call(kernel, out_shape=(shape((256, C), F32), shape((1024, C),...  50.4 us
    pallas_call x1, Pallas kernels, local(): pl.pallas_call(finish, out_shape=(shape((256, C), BF16), shape((1024, C),...  1.27 us

profile of v2, /device:TPU:1, one launch (start us, length us, event | category | flops | bytes accessed | tf_op | source)
XLA Modules:
  0.0 52.3 jit_solution(3695918046567322831)
XLA Ops:
  0.6 50.4 %shard_map.128 = (f32[256,128]{1,0:T(8,128)S(1)}, f32[1024,128]{1,0:T(8,128)S(1)}, bf16[52,16,128]{2,1,0:T(8,128)(2,1)S(1)}, bf16[36,16,128]{2,1,0:T(8,128)(2,1)S(1)}) custom-call(bf16[1024,128]{1,0:T(8,128)(2,1)} %bitcast.8, bf16[256,128]{1,0:T(8,128)(2,1)} %bitcast.9, bf16[1152,128]{1,0:T(8,128)(2,1)} %w1_hbm.1, bf16[1152,128]{1,0:T(8,128)(2,1)} %w2_hbm.1, ...), custom_call_target="tpu_custom_call" | custom-call | tf_op jit(solution)/shard_map/pallas_call | solution.py:593
  51.0 1.3 %shard_map.129 = (bf16[256,128]{1,0:T(8,128)(2,1)}, f32[1024,128]{1,0:T(8,128)}, f32[576,128]{1,0:T(8,128)}, f32[576,128]{1,0:T(8,128)}, f32[256,128]{1,0:T(8,128)}) custom-call(f32[256,128]{1,0:T(8,128)S(1)} %get-tuple-element.14.feat_in, f32[1024,128]{1,0:T(8,128)S(1)} %get-tuple-element.15.ig_in, bf16[52,16,128]{2,1,0:T(8,128)(2,1)S(1)} %get-tuple-element.16.late0, ...), custom_call_target="tpu_custom_call" | custom-call | tf_op jit(solution)/shard_map/pallas_call | solution.py:667

commit v3 on v2

--- a/solution.py
+++ b/solution.py
@@ -383,7 +383,6 @@
             [top[9 * T:], bottom[9 * T:], bottom[:T], top[:T], jnp.zeros((64, C), BF16)], axis=0
         )
         pack(n, mm(rt_mat[...], edges), mm(rct_mat[...], corners))
-        ex_start(n)
 
     def back_centre(wt):
         for a in range(1, 9, 2):
@@ -404,6 +403,7 @@
     for region in EDGE_LINES:
         second_act(region)
     return_rims(2, w2t)
+    ex_start(2)
 
     hid = hid2[...].reshape(4, 2, 4, 2, T, C)
 
@@ -545,8 +545,9 @@
     swap_start(1)
     return_rims(3, w1t)
     scatter_start(1)
+    back_centre(w1t)
+    ex_start(3)
     share_start(0)
-    back_centre(w1t)
     share_start(1)
     add_returned(3)
     ig_ref[...] = flat(inner[...])

time: 52.4 us -> 50.5 us (0.964)
  Pallas kernels: 51.6 us -> 49.7 us
    pallas_call x1, Pallas kernels: 50.4 us -> 48.5 us  [local(): pl.pallas_call(kernel, out_shape=(shape((256, C), F32), shape((1024, C),...]
where the time goes in v3:
time: 50.5 us; the launch traced here: 50.4 us
  Pallas kernels  49.7 us (98%)
  between operations  0.64 us (1%)
    pallas_call x1, Pallas kernels, local(): pl.pallas_call(kernel, out_shape=(shape((256, C), F32), shape((1024, C),...  48.5 us
    pallas_call x1, Pallas kernels, local(): pl.pallas_call(finish, out_shape=(shape((256, C), BF16), shape((1024, C),...  1.27 us

profile of v3, /device:TPU:1, one launch (start us, length us, event | category | flops | bytes accessed | tf_op | source)
XLA Modules:
  0.0 50.4 jit_solution(15686798097679483087)
XLA Ops:
  0.6 48.5 %shard_map.128 = (f32[256,128]{1,0:T(8,128)S(1)}, f32[1024,128]{1,0:T(8,128)S(1)}, bf16[52,16,128]{2,1,0:T(8,128)(2,1)S(1)}, bf16[36,16,128]{2,1,0:T(8,128)(2,1)S(1)}) custom-call(bf16[1024,128]{1,0:T(8,128)(2,1)} %bitcast.8, bf16[256,128]{1,0:T(8,128)(2,1)} %bitcast.9, bf16[1152,128]{1,0:T(8,128)(2,1)} %w1_hbm.1, bf16[1152,128]{1,0:T(8,128)(2,1)} %w2_hbm.1, ...), custom_call_target="tpu_custom_call" | custom-call | tf_op jit(solution)/shard_map/pallas_call | solution.py:594
  49.1 1.3 %shard_map.129 = (bf16[256,128]{1,0:T(8,128)(2,1)}, f32[1024,128]{1,0:T(8,128)}, f32[576,128]{1,0:T(8,128)}, f32[576,128]{1,0:T(8,128)}, f32[256,128]{1,0:T(8,128)}) custom-call(f32[256,128]{1,0:T(8,128)S(1)} %get-tuple-element.14.feat_in, f32[1024,128]{1,0:T(8,128)S(1)} %get-tuple-element.15.ig_in, bf16[52,16,128]{2,1,0:T(8,128)(2,1)S(1)} %get-tuple-element.16.late0, ...), custom_call_target="tpu_custom_call" | custom-call | tf_op jit(solution)/shard_map/pallas_call | solution.py:668

commit v4 on v3

--- a/solution.py
+++ b/solution.py
@@ -98,7 +98,7 @@
     x_ref, cot_ref, w1_ref, w2_ref, wd_ref, eo_ref, co_ref, nb_ref, rot_ref,
     wide, inner, pre1, pre2, pad1, pad2, slope_pad, g_mat, gt_mat, gc_mat, gct_mat,
     r_mat, rt_mat, rc_mat, rct_mat, w1t, w2t, wdt, back6, back2, hid2, cot_p, cot_t,
-    small, gf0, gf1, s_a0, s_a1, r_a0, r_a1, s_b, r_b, s_c, r_c0, r_c1,
+    small, patch_t, gf0, gf1, s_a0, s_a1, r_a0, r_a1, s_b, r_b, s_c, r_c0, r_c1,
     s_edge, r_edge, s_corner, r_corner,
     load_sem, ex_send, ex_recv, red_send, red_recv,
 ):
@@ -343,6 +343,11 @@
     gather(1, pad2)
     ex_start(1)
 
+    def edge_cells(ref, p, q):
+        gap = jnp.zeros((T, C), BF16)
+        sides = [v for j in (q, 7 + q) for v in (gap, flat(ref[1 + p:7 + p, j]), gap)]
+        return jnp.concatenate([flat(ref[p, q:q + 8]), flat(ref[7 + p, q:q + 8])] + sides, axis=0)
+
     conv_centre(pad2, w2_ref, pre2)
 
     def second_act(region):
@@ -352,6 +357,11 @@
         slope_pad[moved(region, 2)] = (back2[region] * (s * (1.0 + v * (1.0 - s)))).astype(BF16)
 
     second_act(INSIDE)
+    for tap, (p, q) in enumerate(TAPS):
+        part = flip(edge_cells(pad1, p, q))
+        for at in range(0, C, 64):
+            row = tap * C + at
+            patch_t[row // 576, row % 576:row % 576 + 64] = part[at:at + 64]
     cot_t[...] = flip(cot_p[...])
     for tap in range(9):
         at = slice(tap * C, tap * C + C)
@@ -410,17 +420,16 @@
     def hid_tap(tap):
         return flat(hid[:, tap // 2, :, tap % 2])
 
-    def put(gf, tap, per_half, at, value, add=False):
+    def put(gf, tap, per_half, at, value):
         value = jnp.transpose(value).reshape(8, 16, C)
         low = tap * 8
         for half in range(2):
             lo, hi = max(low, half * per_half), min(low + 8, (half + 1) * per_half)
             if lo < hi:
                 to = slice(at + lo - half * per_half, at + hi - half * per_half)
-                part = value[lo - low:hi - low]
-                gf[half, to] = gf[half, to] + part if add else part
-
-    def weight_grad(slope_rows, read, gf, add=False):
+                gf[half, to] = value[lo - low:hi - low]
+
+    def weight_grad(slope_rows, read, gf):
         slope_t = flip(slope_rows)
         for a in range(0, 9, 2):
             taps = TAPS[a:a + 2]
@@ -428,7 +437,7 @@
             rhs = rhs[0] if len(rhs) == 1 else jnp.concatenate(rhs, axis=1)
             both = mm(slope_t, rhs)
             for j in range(len(taps)):
-                put(gf, a + j, 36, 0, both[:, j * C:(j + 1) * C], add)
+                put(gf, a + j, 36, 0, both[:, j * C:(j + 1) * C])
 
     for tap in range(4):
         put(gf0, tap, 16, 36, mm(cot_t[...], hid_tap(tap)))
@@ -456,11 +465,6 @@
 
     def swap(n):
         return to_other_core(n, late[n][1], late[n][2], 0)
-
-    def swap_start(n):
-        gf, s_a = late[n][:2]
-        s_a[...] = (gf[1 - core] * GRAD_SCALE).astype(BF16)
-        swap(n).start()
 
     def scatter_start(n):
         gf, _, r_a, _ = late[n]
@@ -517,7 +521,8 @@
         def _():
             many(n, 2, BLOCKS[n]).wait_recv()
 
-    swap_start(0)
+    s_a0[...] = (gf0[1 - core] * GRAD_SCALE).astype(BF16)
+    swap(0).start()
     back_centre(w2t)
     scatter_start(0)
     feats = None
@@ -534,20 +539,22 @@
         flat(slope_pad[3:9, 3:9]), lambda p, q: flat(pad1[1 + p:7 + p, 1 + q:7 + q]), gf1
     )
 
-    def edge_cells(ref, p, q):
-        lines = [ref[p, q:q + 8], ref[7 + p, q:q + 8], ref[1 + p:7 + p, q], ref[1 + p:7 + p, 7 + q]]
-        return jnp.concatenate([flat(v) for v in lines], axis=0)
-
     add_returned(2)
     for region in EDGE_LINES:
         first_slope(region)
-    weight_grad(edge_cells(slope_pad, 2, 2), lambda p, q: edge_cells(pad1, p, q), gf1, add=True)
-    swap_start(1)
+    edge_slopes = edge_cells(slope_pad, 2, 2)
+
+    def first_grad(half):
+        return gf1[half] + mm(patch_t[half], edge_slopes).reshape(36, 16, C)
+
+    s_a1[...] = (first_grad(1 - core) * GRAD_SCALE).astype(BF16)
+    swap(1).start()
     return_rims(3, w1t)
+    gf1[core] = first_grad(core)
     scatter_start(1)
     back_centre(w1t)
+    share_start(0)
     ex_start(3)
-    share_start(0)
     share_start(1)
     add_returned(3)
     ig_ref[...] = flat(inner[...])
@@ -578,13 +585,32 @@
             many(n, 2, N_TILE - 1).wait_send()
 
 
-def finish(feat_in, ig_in, late0, late1, feat_ref, ig_ref, o1_ref, o2_ref, od_ref):
+def finish(
+    feat_in, ig_in, late0, late1, feat_hbm, ig_hbm, o1_hbm, o2_hbm, od_hbm,
+    feat_ref, ig_ref, o1_ref, o2_ref, od_ref, sem,
+):
+    copies = []
+
+    def send(src_ref, dst_ref):
+        copies.append(pltpu.make_async_copy(src_ref, dst_ref, sem.at[len(copies)]))
+        copies[-1].start()
+
+    o2_ref[...] = flat(late0[0:36].astype(F32))
+    send(o2_ref, o2_hbm)
+    o1_ref[...] = flat(late1[...].astype(F32))
+    send(o1_ref, o1_hbm)
+    for t in range(T):
+        ig_ref[pl.ds(t * 64, 64), :] = ig_in[pl.ds(t, 64, stride=T), :]
+        if t % 4 == 3:
+            part = pl.ds((t - 3) * 64, 256)
+            send(ig_ref.at[part], ig_hbm.at[part])
     for t in range(T):
         feat_ref[pl.ds(t * 16, 16), :] = feat_in[pl.ds(t, 16, stride=T), :].astype(BF16)
-        ig_ref[pl.ds(t * 64, 64), :] = ig_in[pl.ds(t, 64, stride=T), :]
-    o1_ref[...] = flat(late1[...].astype(F32))
-    o2_ref[...] = flat(late0[0:36].astype(F32))
+    send(feat_ref, feat_hbm)
     od_ref[...] = flat(late0[36:52].astype(F32))
+    send(od_ref, od_hbm)
+    for copy in copies:
+        copy.wait()
 
 
 def local(inputs, cotangent, w_first, w_second, w_down, edge_owner, corner_owner, neighbour_tile, seam_rotation):
@@ -632,6 +658,7 @@
             v((256, C), BF16),
             v((C, 256), BF16),
             v((256, C), F32),
+            v((2, 576, 512), BF16),
             v((2, 52, 16, C), F32),
             v((2, 36, 16, C), F32),
             v((52, 16, C), BF16),
@@ -672,7 +699,11 @@
             shape((576, C), F32), shape((256, C), F32),
         ),
         in_specs=[vmem] * 4,
-        out_specs=(vmem,) * 5,
+        out_specs=(pl.BlockSpec(memory_space=pltpu.HBM),) * 5,
+        scratch_shapes=[
+            v((256, C), BF16), v((1024, C), F32), v((576, C), F32), v((576, C), F32), v((256, C), F32),
+            pltpu.SemaphoreType.DMA((8,)),
+        ],
         compiler_params=pltpu.CompilerParams(vmem_limit_bytes=16 * 1024 * 1024),
     )(*between)
     return (feats.reshape(1, T, 4, 4, C), grads.reshape(1, T, S, S, C), one, two, low)

time: 50.5 us -> 50.4 us (level)
  no operation moved by 1% of the time
where the time goes in v4:
time: 50.4 us; the launch traced here: 50.3 us
  Pallas kernels  49.4 us (98%)
  between operations  0.8 us (2%)
    pallas_call x1, Pallas kernels, local(): pl.pallas_call(kernel, out_shape=(shape((256, C), F32), shape((1024, C),...  48.3 us
    pallas_call x1, Pallas kernels, local(): pl.pallas_call(finish, out_shape=(shape((256, C), BF16), shape((1024, C),...  1.14 us

profile of v4, /device:TPU:1, one launch (start us, length us, event | category | flops | bytes accessed | tf_op | source)
XLA Modules:
  0.0 50.3 jit_solution(10187441940995107345)
XLA Ops:
  0.6 48.3 %shard_map.128 = (f32[256,128]{1,0:T(8,128)S(1)}, f32[1024,128]{1,0:T(8,128)S(1)}, bf16[52,16,128]{2,1,0:T(8,128)(2,1)S(1)}, bf16[36,16,128]{2,1,0:T(8,128)(2,1)S(1)}) custom-call(bf16[1024,128]{1,0:T(8,128)(2,1)} %bitcast.8, bf16[256,128]{1,0:T(8,128)(2,1)} %bitcast.9, bf16[1152,128]{1,0:T(8,128)(2,1)} %w1_hbm.1, bf16[1152,128]{1,0:T(8,128)(2,1)} %w2_hbm.1, ...), custom_call_target="tpu_custom_call" | custom-call | tf_op jit(solution)/shard_map/pallas_call | solution.py:620
  49.0 1.1 %shard_map.129 = (bf16[256,128]{1,0:T(8,128)(2,1)}, f32[1024,128]{1,0:T(8,128)}, f32[576,128]{1,0:T(8,128)}, f32[576,128]{1,0:T(8,128)}, f32[256,128]{1,0:T(8,128)}) custom-call(f32[256,128]{1,0:T(8,128)S(1)} %get-tuple-element.14.feat_in, f32[1024,128]{1,0:T(8,128)S(1)} %get-tuple-element.15.ig_in, bf16[52,16,128]{2,1,0:T(8,128)(2,1)S(1)} %get-tuple-element.16.late0, ...), custom_call_target="tpu_custom_call" | custom-call | tf_op jit(solution)/shard_map/pallas_call | solution.py:695

commit v5 on v4

--- a/solution.py
+++ b/solution.py
@@ -181,18 +181,25 @@
         line = jnp.where(late, b1, b0) + jnp.where(late, t1, t0) * px
         return jnp.where(valid > 0.5, line * float(T) + jnp.where(late, n1, n0), -1.0)
 
-    te = target(
-        slots_e[0:8],
-        jnp.bitwise_and(jnp.right_shift(lane_i, 3), 1).astype(F32),
-        jnp.bitwise_and(lane_i, 7).astype(F32),
-    )
-    tc = target(slots_c[8:16], jnp.bitwise_and(lane_i[:, :128], 1).astype(F32), 0.0)
+    which_e = jnp.bitwise_and(jnp.right_shift(lane_i, 3), 1).astype(F32)
+    place_e = jnp.bitwise_and(lane_i, 7).astype(F32)
+    which_c = jnp.bitwise_and(lane_i[:, :128], 1).astype(F32)
+    te = target(slots_e[0:8], which_e, place_e)
+    tc = target(slots_c[8:16], which_c, 0.0)
 
     def as_column(row, n):
         return jnp.transpose(jnp.broadcast_to(row, (128, n)))[:, 0:1]
 
-    g_mat[...] = hot(as_column(te, 1024) == lane_f[:, :512])
-    gc_mat[...] = hot(as_column(tc, 128) == lane_f[:, :512])
+    to_e = jnp.zeros((1, 1024), F32)
+    to_c = jnp.zeros((1, 128), F32)
+    for o, rel in enumerate(OFFSETS):
+        ident = peer(rel).astype(F32)
+        to_e = jnp.where(blk_l == float(o), ident, to_e)
+        to_c = jnp.where(jnp.right_shift(lane_i[:, :128], 1).astype(F32) == float(o), ident, to_c)
+    out_e = mm(tab, hot(blk_s == to_e))
+    out_c = mm_nt(tab, hot(as_column(to_c, 128) == blk_l))
+    g_mat[...] = hot(as_column(target(out_e[0:8], which_e, place_e), 1024) == lane_f[:, :512])
+    gc_mat[...] = hot(as_column(target(out_c[8:16], which_c, 0.0), 128) == lane_f[:, :512])
 
     pad1[...] = jnp.zeros_like(pad1)
     loads[4].wait()
@@ -200,14 +207,18 @@
     for px in range(S * S):
         pad1[1 + px // S, 1 + px % S] = wide[pl.ds(px, T, stride=S * S), :].astype(BF16)
 
-    def pack(n, edges, corners):
-        s_edge[n] = edges.astype(BF16).reshape(N_TILE, T, C)
-        s_corner[n] = corners.astype(BF16).reshape(N_TILE, 2, C)
-
-    def gather(n, pad):
+    def pack_send(n, big, edges, little, corners, send):
+        s_corner[n] = mm(little[...], corners).astype(BF16).reshape(N_TILE, 2, C)
+        for part in range(2):
+            rows = mm(big[part * 512:part * 512 + 512], edges)
+            s_edge[n, part * 32:part * 32 + 32] = rows.astype(BF16).reshape(32, T, C)
+            if send:
+                ex_start(n, part)
+
+    def gather(n, pad, send):
         lines = [pad[1, 1:9], pad[8, 1:9], pad[1:9, 1], pad[1:9, 8]]
         lines = jnp.concatenate([flat(v) for v in lines], axis=0)
-        pack(n, mm(g_mat[...], lines), mm(gc_mat[...], lines))
+        pack_send(n, g_mat, lines, gc_mat, lines, send)
 
     def ex_copies(n, src_at, dst_at, d):
         e = pltpu.make_async_remote_copy(
@@ -222,13 +233,14 @@
         )
         return e, c
 
-    def ex_start(n):
-        for rel in PEERS:
-            d = peer(rel)
-            for copy in ex_copies(n, d, me, d):
+    def ex_start(n, part):
+        for o in range(part * 32, min(part * 32 + 32, N_TILE - 1)):
+            d = peer(OFFSETS[o])
+            for copy in ex_copies(n, o, me, d):
                 copy.start()
-        r_edge[n, me] = s_edge[n, me]
-        r_corner[n, me] = s_corner[n, me]
+        if part == 1:
+            r_edge[n, me] = s_edge[n, N_TILE - 1]
+            r_corner[n, me] = s_corner[n, N_TILE - 1]
 
     def ex_all(n):
         rest = pl.ds(0, N_TILE - 1)
@@ -239,9 +251,10 @@
             copy.wait_recv()
         return flat(r_edge[n]), flat(r_corner[n])
 
-    gather(0, pad1)
+    gather(0, pad1, send=False)
     pl.semaphore_wait(barrier, N_TILE)
-    ex_start(0)
+    ex_start(0, 0)
+    ex_start(0, 1)
 
     for load in loads[5:]:
         load.wait()
@@ -340,8 +353,7 @@
     rim_taps(pad1, w1_ref, pre1)
     for region in EDGE_LINES:
         first_act(region)
-    gather(1, pad2)
-    ex_start(1)
+    gather(1, pad2, send=True)
 
     def edge_cells(ref, p, q):
         gap = jnp.zeros((T, C), BF16)
@@ -368,12 +380,13 @@
         w1t[at] = flip(w1_ref[at])
     row_e = jnp.transpose(jnp.broadcast_to(col_e, (512, 128)))[0:1]
     row_c = jnp.transpose(jnp.broadcast_to(col_c, (128, 128)))[0:1]
-    rt_mat[...] = hot(sub_f == row_e)
-    rct_mat[...] = hot(sub_f[:128] == row_c)
+    slot_e = to_e * 16.0 + jnp.bitwise_and(lane_i, 15).astype(F32)
+    rt_mat[...] = hot(as_column(slot_e, 1024) == row_e)
+    rct_mat[...] = hot(as_column(to_c * 2.0 + which_c, 128) == row_c)
     gt_mat[...] = hot(sub_f[:512] == te)
     gct_mat[...] = hot(sub_f[:512] == tc)
 
-    def return_rims(n, wt):
+    def return_rims(n, wt, send):
         rows = []
         for row, p in ((2, 0), (9, 2)):
             lhs = jnp.concatenate([flat(slope_pad[row, 2 - q:12 - q]) for q in range(3)], axis=1)
@@ -392,7 +405,7 @@
         corners = jnp.concatenate(
             [top[9 * T:], bottom[9 * T:], bottom[:T], top[:T], jnp.zeros((64, C), BF16)], axis=0
         )
-        pack(n, mm(rt_mat[...], edges), mm(rct_mat[...], corners))
+        pack_send(n, rt_mat, edges, rct_mat, corners, send)
 
     def back_centre(wt):
         for a in range(1, 9, 2):
@@ -412,8 +425,7 @@
     rim_taps(pad2, w2_ref, pre2)
     for region in EDGE_LINES:
         second_act(region)
-    return_rims(2, w2t)
-    ex_start(2)
+    return_rims(2, w2t, send=True)
 
     hid = hid2[...].reshape(4, 2, 4, 2, T, C)
 
@@ -549,12 +561,13 @@
 
     s_a1[...] = (first_grad(1 - core) * GRAD_SCALE).astype(BF16)
     swap(1).start()
-    return_rims(3, w1t)
+    return_rims(3, w1t, send=False)
     gf1[core] = first_grad(core)
     scatter_start(1)
     back_centre(w1t)
     share_start(0)
-    ex_start(3)
+    ex_start(3, 0)
+    ex_start(3, 1)
     share_start(1)
     add_returned(3)
     ig_ref[...] = flat(inner[...])

time: 50.4 us -> 50.6 us (level)
  no operation moved by 1% of the time
where the time goes in v5:
time: 50.6 us; the launch traced here: 50.5 us
  Pallas kernels  49.7 us (98%)
  between operations  0.8 us (2%)
    pallas_call x1, Pallas kernels, local(): pl.pallas_call(kernel, out_shape=(shape((256, C), F32), shape((1024, C),...  48.5 us
    pallas_call x1, Pallas kernels, local(): pl.pallas_call(finish, out_shape=(shape((256, C), BF16), shape((1024, C),...  1.14 us

profile of v5, /device:TPU:1, one launch (start us, length us, event | category | flops | bytes accessed | tf_op | source)
XLA Modules:
  0.0 50.5 jit_solution(209788819221060271)
XLA Ops:
  0.6 48.5 %shard_map.128 = (f32[256,128]{1,0:T(8,128)S(1)}, f32[1024,128]{1,0:T(8,128)S(1)}, bf16[52,16,128]{2,1,0:T(8,128)(2,1)S(1)}, bf16[36,16,128]{2,1,0:T(8,128)(2,1)S(1)}) custom-call(bf16[1024,128]{1,0:T(8,128)(2,1)} %bitcast.8, bf16[256,128]{1,0:T(8,128)(2,1)} %bitcast.9, bf16[1152,128]{1,0:T(8,128)(2,1)} %w1_hbm.1, bf16[1152,128]{1,0:T(8,128)(2,1)} %w2_hbm.1, ...), custom_call_target="tpu_custom_call" | custom-call | tf_op jit(solution)/shard_map/pallas_call | solution.py:633
  49.2 1.1 %shard_map.129 = (bf16[256,128]{1,0:T(8,128)(2,1)}, f32[1024,128]{1,0:T(8,128)}, f32[576,128]{1,0:T(8,128)}, f32[576,128]{1,0:T(8,128)}, f32[256,128]{1,0:T(8,128)}) custom-call(f32[256,128]{1,0:T(8,128)S(1)} %get-tuple-element.14.feat_in, f32[1024,128]{1,0:T(8,128)S(1)} %get-tuple-element.15.ig_in, bf16[52,16,128]{2,1,0:T(8,128)(2,1)S(1)} %get-tuple-element.16.late0, ...), custom_call_target="tpu_custom_call" | custom-call | tf_op jit(solution)/shard_map/pallas_call | solution.py:708
